TPU v7x, 32 devices: a whole 2x2x4 slice. The times are simulated.
32 devices in a mesh: group: 16 (over z, x, core), fsdp: 2 (over y).
Axes of the slice: x: 2, y: 2, z: 4, core: 2. Of those that a mesh axis runs over, the one named last changes fastest.
Arguments:
- inputs: bfloat16 [32, 1024, 1152], P('group', 'fsdp'), may hold values from -6 to 6
- segments: int32 [32, 1024], P('group'), may hold values from 0 to 3, never falling along the last dimension, each value on 1 to 768 neighbouring positions
- out_grad: bfloat16 [32, 1024, 1152], P('group', 'fsdp'), may hold values from -6 to 6
- attention_gain: bfloat16 [1152], P('fsdp'), may hold values from 0.5 to 1.5
- query_weight: bfloat16 [1152, 1152], P('fsdp'), may hold values from -0.1875 to 0.1875
- key_weight: bfloat16 [1152, 384], P('fsdp'), may hold values from -0.1875 to 0.1875
- value_weight: bfloat16 [1152, 384], P('fsdp'), may hold values from -0.1875 to 0.1875
- output_weight: bfloat16 [1152, 1152], P('fsdp'), may hold values from -1 to 1
- feedforward_gain: bfloat16 [1152], P('fsdp'), may hold values from 0.5 to 1.5
- gate_weight: bfloat16 [1152, 3072], P('fsdp'), may hold values from -0.1875 to 0.1875
- up_weight: bfloat16 [1152, 3072], P('fsdp'), may hold values from -0.1875 to 0.1875
- down_weight: bfloat16 [3072, 1152], P('fsdp'), may hold values from -0.109375 to 0.109375
Outputs:
- output: bfloat16 [32, 1024, 1152], P('group', 'fsdp')
- input_grad: bfloat16 [32, 1024, 1152], P('group', 'fsdp')
- attention_gain_grad: float32 [1152], P('fsdp')
- query_weight_grad: float32 [1152, 1152], P('fsdp')
- key_weight_grad: float32 [1152, 384], P('fsdp')
- value_weight_grad: float32 [1152, 384], P('fsdp')
- output_weight_grad: float32 [1152, 1152], P('fsdp')
- feedforward_gain_grad: float32 [1152], P('fsdp')
- gate_weight_grad: float32 [1152, 3072], P('fsdp')
- up_weight_grad: float32 [1152, 3072], P('fsdp')
- down_weight_grad: float32 [3072, 1152], P('fsdp')
All inputs are finite; a program needn't handle non-finite values.
Results may differ from a plain program's by a relative error of at most 0.015.
Values may be sent and summed in bfloat16 or wider, within the bound.
A program may use at most 448 MiB of HBM per device.

v0:
```python
import math

import jax
import jax.numpy as jnp
from jax import lax
from jax.sharding import PartitionSpec as P

HEADS = 18
KV_HEADS = 6
HEAD = 64


epsilon = 1e-05
rope_base = 10000.0


def shortened(array):
    return jax.tree.map(lambda a: a.astype(jnp.bfloat16) if a.dtype == jnp.float32 else a, array)


def product(left, right):
    return jnp.dot(left, right, preferred_element_type=jnp.float32)


def product_tn(left, right):
    return lax.dot_general(
        left, right, (((0,), (0,)), ((), ())), preferred_element_type=jnp.float32
    )


def product_nt(left, right):
    return lax.dot_general(
        left, right, (((1,), (1,)), ((), ())), preferred_element_type=jnp.float32
    )


def rotary_tables(positions, width):
    half_width = width // 2
    freqs = jnp.exp(
        jnp.arange(half_width, dtype=jnp.float32) * (-2.0 * math.log(rope_base) / width)
    )
    angles = positions[:, None] * freqs[None, :]
    return (jnp.cos(angles), jnp.sin(angles))


def rotate(values, cosines, sines):
    half_width = values.shape[-1] // 2
    first = values[..., :half_width]
    second = values[..., half_width:]
    return jnp.concatenate(
        [first * cosines - second * sines, second * cosines + first * sines], axis=-1
    )


def unrotate(values, cosines, sines):
    half_width = values.shape[-1] // 2
    first = values[..., :half_width]
    second = values[..., half_width:]
    return jnp.concatenate(
        [first * cosines + second * sines, second * cosines - first * sines], axis=-1
    )


def norm_back(grad_rows, gain, scaled, inverse):
    weighted = grad_rows * gain
    return inverse * (weighted - scaled * jnp.mean(weighted * scaled, axis=-1, keepdims=True))


def local(
    inputs,
    segments,
    out_grad,
    attention_gain,
    query_weight,
    key_weight,
    value_weight,
    output_weight,
    feedforward_gain,
    gate_weight,
    up_weight,
    down_weight,
):
    gathered = (
        lax.all_gather(attention_gain, "fsdp", axis=0, tiled=True),
        lax.all_gather(query_weight, "fsdp", axis=0, tiled=True),
        lax.all_gather(key_weight, "fsdp", axis=0, tiled=True),
        lax.all_gather(value_weight, "fsdp", axis=0, tiled=True),
        lax.all_gather(output_weight, "fsdp", axis=0, tiled=True),
        lax.all_gather(feedforward_gain, "fsdp", axis=0, tiled=True),
        lax.all_gather(gate_weight, "fsdp", axis=0, tiled=True),
        lax.all_gather(up_weight, "fsdp", axis=0, tiled=True),
        lax.all_gather(down_weight, "fsdp", axis=0, tiled=True),
    )
    full_query, full_key, full_value, full_output = (
        gathered[1],
        gathered[2],
        gathered[3],
        gathered[4],
    )
    full_gate, full_up, full_down = (gathered[6], gathered[7], gathered[8])
    gain_attention = gathered[0].astype(jnp.float32)
    gain_feed = gathered[5].astype(jnp.float32)
    span = inputs.shape[1]
    length = segments.shape[1]
    groups_q = HEADS // KV_HEADS
    key_width = KV_HEADS * HEAD
    start = lax.axis_index("fsdp") * span
    query_pos = start + jnp.arange(span, dtype=jnp.int32)
    key_pos = jnp.arange(length, dtype=jnp.int32)
    cosines, sines = rotary_tables(query_pos.astype(jnp.float32), HEAD)
    cos_four, sin_four = (cosines[:, None, None, :], sines[:, None, None, :])
    cos_three, sin_three = (cosines[:, None, :], sines[:, None, :])
    causal = query_pos[:, None] >= key_pos[None, :]
    scale = HEAD ** (-0.5)

    def micro_step(totals, sequence):
        tokens, segment_row, cotangent = sequence
        own_segment = lax.dynamic_slice_in_dim(segment_row, start, span)
        allowed = causal & (own_segment[:, None] == segment_row[None, :])
        values = tokens.astype(jnp.float32)
        inverse_a = lax.rsqrt(jnp.mean(values * values, axis=-1, keepdims=True) + epsilon)
        scaled_a = values * inverse_a
        normed_a = (scaled_a * gain_attention).astype(jnp.bfloat16)
        query_lin = product(normed_a, full_query).reshape(span, KV_HEADS, groups_q, HEAD)
        queries = rotate(query_lin, cos_four, sin_four).astype(jnp.bfloat16)
        key_lin = product(normed_a, full_key).reshape(span, KV_HEADS, HEAD)
        key_rows = (
            rotate(key_lin, cos_three, sin_three).astype(jnp.bfloat16).reshape(span, key_width)
        )
        value_rows = product(normed_a, full_value).astype(jnp.bfloat16)
        all_keys, all_values = (
            lax.all_gather(key_rows, "fsdp", axis=0, tiled=True),
            lax.all_gather(value_rows, "fsdp", axis=0, tiled=True),
        )
        all_keys = all_keys.reshape(length, KV_HEADS, HEAD)
        all_values = all_values.reshape(length, KV_HEADS, HEAD)
        scores = (
            jnp.einsum("qhgd,khd->hgqk", queries, all_keys, preferred_element_type=jnp.float32)
            * scale
        )
        scores = jnp.where(allowed, scores, -1e30)
        highest = jnp.max(scores, axis=-1, keepdims=True)
        expo_scores = jnp.exp(scores - highest)
        attention = expo_scores / jnp.sum(expo_scores, axis=-1, keepdims=True)
        attention_low = attention.astype(jnp.bfloat16)
        mixed = jnp.einsum(
            "hgqk,khd->qhgd", attention_low, all_values, preferred_element_type=jnp.float32
        )
        mixed = mixed.reshape(span, HEADS * HEAD).astype(jnp.bfloat16)
        residual = values + product(mixed, full_output)
        inverse_f = lax.rsqrt(jnp.mean(residual * residual, axis=-1, keepdims=True) + epsilon)
        scaled_f = residual * inverse_f
        normed_f = (scaled_f * gain_feed).astype(jnp.bfloat16)
        gate_sum = product(normed_f, full_gate)
        up_sum = product(normed_f, full_up)
        sigmoid_gate = jax.nn.sigmoid(gate_sum)
        activated = gate_sum * sigmoid_gate
        hidden = (activated * up_sum).astype(jnp.bfloat16)
        result = (residual + product(hidden, full_down)).astype(jnp.bfloat16)
        down_wgrad = product_tn(hidden, cotangent)
        hidden_grad = product_nt(cotangent, full_down)
        gate_grad = (
            hidden_grad * up_sum * sigmoid_gate * (1.0 + gate_sum * (1.0 - sigmoid_gate))
        ).astype(jnp.bfloat16)
        up_grad = (hidden_grad * activated).astype(jnp.bfloat16)
        gate_wgrad = product_tn(normed_f, gate_grad)
        up_wgrad = product_tn(normed_f, up_grad)
        normed_f_grad = product_nt(gate_grad, full_gate) + product_nt(up_grad, full_up)
        feed_gain_grad = jnp.sum(normed_f_grad * scaled_f, axis=0)
        residual_grad = cotangent.astype(jnp.float32) + norm_back(
            normed_f_grad, gain_feed, scaled_f, inverse_f
        )
        residual_low = residual_grad.astype(jnp.bfloat16)
        output_wgrad = product_tn(mixed, residual_low)
        mixed_grad = (
            product_nt(residual_low, full_output)
            .astype(jnp.bfloat16)
            .reshape(span, KV_HEADS, groups_q, HEAD)
        )
        attention_grad = jnp.einsum(
            "qhgd,khd->hgqk", mixed_grad, all_values, preferred_element_type=jnp.float32
        )
        row_totals = jnp.sum(attention * attention_grad, axis=-1, keepdims=True)
        score_grad = (attention * (attention_grad - row_totals) * scale).astype(jnp.bfloat16)
        value_grads = jnp.einsum(
            "hgqk,qhgd->khd", attention_low, mixed_grad, preferred_element_type=jnp.float32
        ).reshape(length, key_width)
        key_grads = jnp.einsum(
            "hgqk,qhgd->khd", score_grad, queries, preferred_element_type=jnp.float32
        ).reshape(length, key_width)
        query_grad = jnp.einsum(
            "hgqk,khd->qhgd", score_grad, all_keys, preferred_element_type=jnp.float32
        )
        key_back, value_back = (
            lax.psum_scatter(key_grads, "fsdp", scatter_dimension=0, tiled=True),
            lax.psum_scatter(value_grads, "fsdp", scatter_dimension=0, tiled=True),
        )
        query_low = (
            unrotate(query_grad, cos_four, sin_four)
            .reshape(span, HEADS * HEAD)
            .astype(jnp.bfloat16)
        )
        key_low = (
            unrotate(key_back.reshape(span, KV_HEADS, HEAD), cos_three, sin_three)
            .reshape(span, key_width)
            .astype(jnp.bfloat16)
        )
        value_low = value_back.astype(jnp.bfloat16)
        query_wgrad = product_tn(normed_a, query_low)
        key_wgrad = product_tn(normed_a, key_low)
        value_wgrad = product_tn(normed_a, value_low)
        normed_a_grad = (
            product_nt(query_low, full_query)
            + product_nt(key_low, full_key)
            + product_nt(value_low, full_value)
        )
        attention_gain_term = jnp.sum(normed_a_grad * scaled_a, axis=0)
        token_grad = (
            residual_grad + norm_back(normed_a_grad, gain_attention, scaled_a, inverse_a)
        ).astype(jnp.bfloat16)
        terms = (
            attention_gain_term,
            query_wgrad,
            key_wgrad,
            value_wgrad,
            output_wgrad,
            feed_gain_grad,
            gate_wgrad,
            up_wgrad,
            down_wgrad,
        )
        totals = tuple((left + right for left, right in zip(totals, terms)))
        return (totals, (result, token_grad))

    initial = tuple((jnp.zeros(weight.shape, jnp.float32) for weight in gathered))
    totals, (outputs, input_grads) = lax.scan(micro_step, initial, (inputs, segments, out_grad))
    shards = jax.tree.map(
        lambda part: part.astype(jnp.float32),
        lax.psum_scatter(shortened(totals), "fsdp", scatter_dimension=0, tiled=True),
    )
    summed = lax.psum(shards, "group")
    return (
        outputs,
        input_grads,
        summed[0],
        summed[1],
        summed[2],
        summed[3],
        summed[4],
        summed[5],
        summed[6],
        summed[7],
        summed[8],
    )


def solution(mesh):
    placed = (
        P("group", "fsdp", None),
        P("group", None),
        P("group", "fsdp", None),
        P("fsdp"),
        P("fsdp", None),
        P("fsdp", None),
        P("fsdp", None),
        P("fsdp", None),
        P("fsdp"),
        P("fsdp", None),
        P("fsdp", None),
        P("fsdp", None),
    )
    return jax.shard_map(
        local,
        mesh=mesh,
        in_specs=placed,
        out_specs=(
            P("group", "fsdp", None),
            P("group", "fsdp", None),
            P("fsdp"),
            P("fsdp", None),
            P("fsdp", None),
            P("fsdp", None),
            P("fsdp", None),
            P("fsdp"),
            P("fsdp", None),
            P("fsdp", None),
            P("fsdp", None),
        ),
        check_vma=False,
    )
```

profile of v0, /device:TPU:0, one launch (start us, length us, event | category | flops | bytes accessed | tf_op | source)
XLA Modules:
  0.0 2013.0 jit_solution(825996235863366552)
XLA Ops:
  18.5 21.4 %all_gather.42 = bf16[1152,384]{1,0:T(8,128)(2,1)S(1)} all-gather(bf16[576,384]{1,0:T(8,128)(2,1)S(1)} %copy-done.42), channel_id=1, replica_groups=mesh['group'=16,'fsdp'=2] {'fsdp'}, dimensions={0}, use_global_device_ids=true | all-gather | bytes 1327104 | tf_op jit(solution)/shard_map/all_gather | solution.py:86
  41.4 22.2 %all_gather.44 = bf16[1152,384]{1,0:T(8,128)(2,1)S(1)} all-gather(bf16[576,384]{1,0:T(8,128)(2,1)S(1)} %copy-done.43), channel_id=1, replica_groups=mesh['group'=16,'fsdp'=2] {'fsdp'}, dimensions={0}, use_global_device_ids=true | all-gather | bytes 1327104 | tf_op jit(solution)/shard_map/all_gather | solution.py:87
  73.6 37.2 %all-gather.8.cloned.1.call-done = bf16[1152,1152]{1,0:T(8,128)(2,1)} async-done(((bf16[576,1152]{1,0:T(8,128)(2,1)}), bf16[1152,1152]{1,0:T(8,128)(2,1)}) %all-gather.8.cloned.1.call-update) | async-done | bytes 2654224 | tf_op jit(solution)/shard_map/all_gather | solution.py:88
  110.8 90.8 %all-gather.14.cloned.1.call-done = bf16[1152,3072]{1,0:T(8,128)(2,1)} async-done(((bf16[576,3072]{1,0:T(8,128)(2,1)}), bf16[1152,3072]{1,0:T(8,128)(2,1)}) %all-gather.14.cloned.1.call-update) | async-done | bytes 7077904 | tf_op jit(solution)/shard_map/all_gather | solution.py:90
  201.6 90.6 %all-gather.12.cloned.1.call-done = bf16[1152,3072]{1,0:T(8,128)(2,1)} async-done(((bf16[576,3072]{1,0:T(8,128)(2,1)}), bf16[1152,3072]{1,0:T(8,128)(2,1)}) %all-gather.12.cloned.1.call-update) | async-done | bytes 7077904 | tf_op jit(solution)/shard_map/all_gather | solution.py:91
  292.2 90.6 %all-gather.10.cloned.1.call-done = bf16[3072,1152]{1,0:T(8,128)(2,1)} async-done(((bf16[1536,1152]{1,0:T(8,128)(2,1)}), bf16[3072,1152]{1,0:T(8,128)(2,1)}) %all-gather.10.cloned.1.call-update) | async-done | bytes 7077904 | tf_op jit(solution)/shard_map/all_gather | solution.py:92
  382.9 651.1 %while.36 = (s32[]{:T(128)}, f32[1152]{0:T(1024)}, f32[1152,1152]{1,0:T(8,128)}, f32[1152,384]{1,0:T(8,128)}, f32[1152,384]{1,0:T(8,128)}, /*index=5*/f32[1152,1...) while((s32[]{:T(128)}, f32[1152]{0:T(1024)}, ...), condition=%wide.region_12.13_spmd.clone.clone.clone, body=%wide.region_0.12_spmd.clone.clone.clone.sunk | while | flops 51052863488 | bytes 1019911296 | solution.py:236
  419.3 19.7 fusion.263
  439.0 13.8 fusion.264
  506.4 14.7 fusion.268
  521.2 48.4 %fusion.271 = f32[6,64,1024,1]{2,1,3,0:T(8,128)} fusion(f32[6,1024,512,3]{2,1,3,0:T(8,128)} %fusion.268, bf16[512,6,3,32]{0,3,2,1:T(8,128)(2,1)S(1)} %copy-done.33, bf16[512,6,3,32]{0,3,2,1:T(8,128)(2,1)S(1)} %copy-done.32, f32[6,3,512,1024]{2,3,1,0:T(8,128)} %get-tuple-element.1056, f32[6,3,512]{2,1,0:T(4,128)S(1)} %get-tuple-element.1057), kind=kOutput, calls=%fused_computation.21.clone.1 | convolution fusion | flops 1276389376 | bytes 78286848 | tf_op jit(solution)/shard_map/while/body/eval_jaxpr/hgqk,qhgd->khd/dot_general | solution.py:188
  569.7 16.6 fusion.272
  586.3 49.2 %fusion.269 = f32[512,6,3,64]{0,3,2,1:T(8,128)} fusion(bf16[1024,6,64,1]{0,2,3,1:T(8,128)(2,1)S(1)} %bitcast.352, f32[6,1024,512,3]{2,1,3,0:T(8,128)} %fusion.268, f32[6,3,512,1024]{2,3,1,0:T(8,128)} %get-tuple-element.1056, f32[6,3,512]{2,1,0:T(4,128)S(1)} %get-tuple-element.1057), kind=kOutput, calls=%fused_computation.74.clone.1 | convolution fusion | flops 1274030080 | bytes 78680064 | tf_op jit(solution)/shard_map/while/body/eval_jaxpr/hgqk,khd->qhgd/dot_general | solution.py:191
  734.9 19.6 fusion.263
  821.7 14.7 fusion.268
  836.5 48.4 %fusion.271 = f32[6,64,1024,1]{2,1,3,0:T(8,128)} fusion(f32[6,1024,512,3]{2,1,3,0:T(8,128)} %fusion.268, bf16[512,6,3,32]{0,3,2,1:T(8,128)(2,1)S(1)} %copy-done.33, bf16[512,6,3,32]{0,3,2,1:T(8,128)(2,1)S(1)} %copy-done.32, f32[6,3,512,1024]{2,3,1,0:T(8,128)} %get-tuple-element.1056, f32[6,3,512]{2,1,0:T(4,128)S(1)} %get-tuple-element.1057), kind=kOutput, calls=%fused_computation.21.clone.1 | convolution fusion | flops 1276389376 | bytes 78286848 | tf_op jit(solution)/shard_map/while/body/eval_jaxpr/hgqk,qhgd->khd/dot_general | solution.py:188
  885.0 16.6 fusion.272
  901.6 49.2 %fusion.269 = f32[512,6,3,64]{0,3,2,1:T(8,128)} fusion(bf16[1024,6,64,1]{0,2,3,1:T(8,128)(2,1)S(1)} %bitcast.352, f32[6,1024,512,3]{2,1,3,0:T(8,128)} %fusion.268, f32[6,3,512,1024]{2,3,1,0:T(8,128)} %get-tuple-element.1056, f32[6,3,512]{2,1,0:T(4,128)S(1)} %get-tuple-element.1057), kind=kOutput, calls=%fused_computation.74.clone.1 | convolution fusion | flops 1274030080 | bytes 78680064 | tf_op jit(solution)/shard_map/while/body/eval_jaxpr/hgqk,khd->qhgd/dot_general | solution.py:191
  1079.8 38.5 %reduce-scatter.10.cloned.1.call-done = bf16[576,1152]{1,0:T(8,128)(2,1)} async-done(((bf16[1152,1152]{1,0:T(8,128)(2,1)}), bf16[576,1152]{1,0:T(8,128)(2,1)}) %reduce-scatter.10.cloned.1.call-update) | async-done | bytes 1327120 | tf_op jit(solution)/shard_map/reduce_scatter | solution.py:239
  1118.3 40.9 %reduce-scatter.16.cloned.1.call-done = bf16[576,1152]{1,0:T(8,128)(2,1)} async-done(((bf16[1152,1152]{1,0:T(8,128)(2,1)}), bf16[576,1152]{1,0:T(8,128)(2,1)}) %reduce-scatter.16.cloned.1.call-update) | async-done | bytes 1327120 | tf_op jit(solution)/shard_map/reduce_scatter | solution.py:239
  1159.2 88.4 %reduce-scatter.18.cloned.1.call-done = bf16[576,3072]{1,0:T(8,128)(2,1)} async-done(((bf16[1152,3072]{1,0:T(8,128)(2,1)}), bf16[576,3072]{1,0:T(8,128)(2,1)}) %reduce-scatter.18.cloned.1.call-update) | async-done | bytes 3538960 | tf_op jit(solution)/shard_map/reduce_scatter | solution.py:239
  1247.6 88.4 %reduce-scatter.20.cloned.1.call-done = bf16[576,3072]{1,0:T(8,128)(2,1)} async-done(((bf16[1152,3072]{1,0:T(8,128)(2,1)}), bf16[576,3072]{1,0:T(8,128)(2,1)}) %reduce-scatter.20.cloned.1.call-update) | async-done | bytes 3538960 | tf_op jit(solution)/shard_map/reduce_scatter | solution.py:239
  1336.0 88.4 %reduce-scatter.22.cloned.1.call-done = bf16[1536,1152]{1,0:T(8,128)(2,1)} async-done(((bf16[3072,1152]{1,0:T(8,128)(2,1)}), bf16[1536,1152]{1,0:T(8,128)(2,1)}) %reduce-scatter.22.cloned.1.call-update) | async-done | bytes 3538960 | tf_op jit(solution)/shard_map/reduce_scatter | solution.py:239
  1424.4 581.8 %all-reduce.8 = (f32[576]{0:T(1024)}, f32[576,1152]{1,0:T(8,128)}, f32[576,384]{1,0:T(8,128)}, f32[576,384]{1,0:T(8,128)}, f32[576,1152]{1,0:T(8,128)}, /*index=...) all-reduce(f32[576]{0:T(1024)S(1)} %dynamic-slice_convert_fusion.1,, ...), channel_id=1, replica_groups=mesh['group'=16,'fsdp'=2] {'group'}, use_global_device_ids=true, to_apply=%region_14.15 | all-reduce | flops 7079040 | bytes 42476544 | tf_op jit(solution)/shard_map/psum | solution.py:241
  (423 shorter events, 400.7 us)
Async XLA Ops:
  7.2 61.2 %all-gather.6.cloned.1.call-start = ((), (), s32[]{:S(2)}) async-start(), calls=%async_computation.9 | async-start | bytes 3981312 | tf_op jit(solution)/shard_map/all_gather | solution.py:85
  7.9 102.9 %all-gather.8.cloned.1.call-start = ((), (), s32[]{:S(2)}) async-start(), calls=%async_computation.10 | async-start | bytes 3981312 | tf_op jit(solution)/shard_map/all_gather | solution.py:88
  8.7 192.9 %all-gather.14.cloned.1.call-start = ((), (), s32[]{:S(2)}) async-start(), calls=%async_computation.13 | async-start | bytes 10616832 | tf_op jit(solution)/shard_map/all_gather | solution.py:90
  9.4 282.8 %all-gather.12.cloned.1.call-start = ((), (), s32[]{:S(2)}) async-start(), calls=%async_computation.12 | async-start | bytes 10616832 | tf_op jit(solution)/shard_map/all_gather | solution.py:91
  10.0 372.9 %all-gather.10.cloned.1.call-start = ((), (), s32[]{:S(2)}) async-start(), calls=%async_computation.11 | async-start | bytes 10616832 | tf_op jit(solution)/shard_map/all_gather | solution.py:92
  63.6 319.2 %copy-start = (bf16[2,512,1152]{2,1,0:T(8,128)(2,1)S(1)}, bf16[2,512,1152]{2,1,0:T(8,128)(2,1)}, u32[]{:S(2)}) copy-start(bf16[2,512,1152]{2,1,0:T(8,128)(2,1)} %param.14) | copy-start | bytes 7077892
  382.9 118.7 %copy-start.40 = (f32[1152]{0:T(1024)}, f32[1152]{0:T(1024)S(1)}, u32[]{:S(2)}) copy-start(f32[1152]{0:T(1024)S(1)} %get-tuple-element.1155) | copy-start | bytes 13828 | tf_op jit(solution)/shard_map/while
  382.9 304.0 %reduce-scatter.24.cloned.1.call-start = ((), (), s32[]{:S(2)}) async-start(), calls=%async_computation.21 | async-start | bytes 2359296 | tf_op jit(solution)/shard_map/while/body/eval_jaxpr/reduce_scatter | solution.py:195
  383.6 32.7 %copy-start.30 = (f32[512,32]{0,1:T(8,128)}, f32[512,32]{0,1:T(8,128)S(1)}, u32[]{:S(2)}) copy-start(f32[512,32]{0,1:T(8,128)S(1)} %get-tuple-element.1053) | copy-start | bytes 196612 | tf_op jit(solution)/shard_map/while
  457.2 44.4 %copy-start.3 = (f32[512,1152]{1,0:T(8,128)}, f32[512,1152]{1,0:T(8,128)S(1)}, u32[]{:S(2)}) copy-start(f32[512,1152]{1,0:T(8,128)S(1)} %get-tuple-element.1058) | copy-start | bytes 7077892 | tf_op jit(solution)/shard_map/while
  569.6 124.0 %reduce-scatter.26.cloned.1.call-start = ((), (), s32[]{:S(2)}) async-start(), calls=%async_computation.22 | async-start | bytes 2359296 | tf_op jit(solution)/shard_map/while/body/eval_jaxpr/reduce_scatter | solution.py:196
  586.3 49.2 %copy-start.4 = (f32[512,1152]{1,0:T(8,128)S(1)}, f32[512,1152]{1,0:T(8,128)}, u32[]{:S(2)}) copy-start(f32[512,1152]{1,0:T(8,128)} %copy-done.3) | copy-start | bytes 7077892 | tf_op jit(solution)/shard_map/while
  701.9 115.0 %copy-start.40 = (f32[1152]{0:T(1024)}, f32[1152]{0:T(1024)S(1)}, u32[]{:S(2)}) copy-start(f32[1152]{0:T(1024)S(1)} %get-tuple-element.1155) | copy-start | bytes 13828 | tf_op jit(solution)/shard_map/while
  701.9 311.8 %reduce-scatter.24.cloned.1.call-start = ((), (), s32[]{:S(2)}) async-start(), calls=%async_computation.21 | async-start | bytes 2359296 | tf_op jit(solution)/shard_map/while/body/eval_jaxpr/reduce_scatter | solution.py:195
  772.6 44.3 %copy-start.3 = (f32[512,1152]{1,0:T(8,128)}, f32[512,1152]{1,0:T(8,128)S(1)}, u32[]{:S(2)}) copy-start(f32[512,1152]{1,0:T(8,128)S(1)} %get-tuple-element.1058) | copy-start | bytes 7077892 | tf_op jit(solution)/shard_map/while
  884.9 136.3 %reduce-scatter.26.cloned.1.call-start = ((), (), s32[]{:S(2)}) async-start(), calls=%async_computation.22 | async-start | bytes 2359296 | tf_op jit(solution)/shard_map/while/body/eval_jaxpr/reduce_scatter | solution.py:196
  901.6 49.2 %copy-start.4 = (f32[512,1152]{1,0:T(8,128)S(1)}, f32[512,1152]{1,0:T(8,128)}, u32[]{:S(2)}) copy-start(f32[512,1152]{1,0:T(8,128)} %copy-done.3) | copy-start | bytes 7077892 | tf_op jit(solution)/shard_map/while
  1034.0 45.8 %reduce-scatter.12.cloned.1.call-start = ((), (), s32[]{:S(2)}) async-start(), calls=%async_computation.15 | async-start | bytes 1327104 | tf_op jit(solution)/shard_map/reduce_scatter | solution.py:239
  1036.7 43.1 %reduce-scatter.14.cloned.1.call-start = ((), (), s32[]{:S(2)}) async-start(), calls=%async_computation.16 | async-start | bytes 1327104 | tf_op jit(solution)/shard_map/reduce_scatter | solution.py:239
  1037.8 80.5 %reduce-scatter.10.cloned.1.call-start = ((), (), s32[]{:S(2)}) async-start(), calls=%async_computation.14 | async-start | bytes 3981312 | tf_op jit(solution)/shard_map/reduce_scatter | solution.py:239
  1042.1 117.0 %reduce-scatter.16.cloned.1.call-start = ((), (), s32[]{:S(2)}) async-start(), calls=%async_computation.17 | async-start | bytes 3981312 | tf_op jit(solution)/shard_map/reduce_scatter | solution.py:239
  1046.8 200.8 %reduce-scatter.18.cloned.1.call-start = ((), (), s32[]{:S(2)}) async-start(), calls=%async_computation.18 | async-start | bytes 10616832 | tf_op jit(solution)/shard_map/reduce_scatter | solution.py:239
  1056.0 280.0 %reduce-scatter.20.cloned.1.call-start = ((), (), s32[]{:S(2)}) async-start(), calls=%async_computation.19 | async-start | bytes 10616832 | tf_op jit(solution)/shard_map/reduce_scatter | solution.py:239
  1065.2 359.3 %reduce-scatter.22.cloned.1.call-start = ((), (), s32[]{:S(2)}) async-start(), calls=%async_computation.20 | async-start | bytes 10616832 | tf_op jit(solution)/shard_map/reduce_scatter | solution.py:239
  (117 other events, 992.4 us)
Sparse Core Ops, SparseCore 0:
  9.5 58.8 all-gather.5
  69.9 40.8 all-gather.7
  112.4 89.2 all-gather.13
  203.0 89.2 all-gather.11
  293.6 89.2 all-gather.9
  569.7 26.1 reduce-scatter.23
  598.2 26.1 reduce-scatter.25
  885.0 26.2 reduce-scatter.23
  913.5 26.1 reduce-scatter.25
  1037.4 18.5 reduce-scatter.11
  1058.8 18.6 reduce-scatter.13
  1080.2 38.0 reduce-scatter.9
  1121.1 38.0 reduce-scatter.15
  1161.9 85.6 reduce-scatter.17
  1250.3 85.6 reduce-scatter.19
  1338.8 85.6 reduce-scatter.21
where the time goes:
time: 2030 us; the launch traced here: 2010 us
  blocking collectives  677 us (33%)
  waiting for transfers between devices  662 us (33%)
  matrix products  564 us (28%)
  other arithmetic  61 us (3%)
  local copies, waits for them, and re-layouts  26.4 us (1%)
    psum x1, blocking collectives, local(): summed = lax.psum(shards, 'group')  582 us
    reduce_scatter x7, waiting for transfers between devices, local(): lax.psum_scatter(shortened(totals), 'fsdp', scatter_dimension=0, tiled=True)  345 us
    dot_general x2, matrix products, micro_step(): jnp.einsum('hgqk,khd->qhgd', score_grad, all_keys, preferred_element_type...  98.4 us
    dot_general x2, matrix products, micro_step(): jnp.einsum('hgqk,qhgd->khd', score_grad, queries, preferred_element_type=...  96.8 us
    all_gather x1, waiting for transfers between devices, local(): lax.all_gather(gate_weight, 'fsdp', axis=0, tiled=True)  90.8 us
    all_gather x1, waiting for transfers between devices, local(): lax.all_gather(up_weight, 'fsdp', axis=0, tiled=True)  90.6 us
    all_gather x1, waiting for transfers between devices, local(): lax.all_gather(down_weight, 'fsdp', axis=0, tiled=True)  90.6 us
    dot_general x14, matrix products, product_tn(): lax.dot_general(left, right, (((0,), (0,)), ((), ())), preferred_element_...  90.1 us
  transfers between devices with their start and end apart: 16, of which 10 were waited for; matrix products, arithmetic and copies ran while one was open for 15% of the time, Pallas kernels for 0%

commit v1 on v0

--- a/solution.py
+++ b/solution.py
@@ -1,17 +1,437 @@
+import functools
 import math
 
 import jax
 import jax.numpy as jnp
 from jax import lax
+from jax.experimental import pallas as pl
+from jax.experimental.pallas import tpu as pltpu
 from jax.sharding import PartitionSpec as P
 
 HEADS = 18
 KV_HEADS = 6
 HEAD = 64
-
-
 epsilon = 1e-05
 rope_base = 10000.0
+BLOCK = 256
+WIDE = 128
+VMEM_MOST = 66 * 1024 * 1024 - 3 * 1024 * 1024
+
+
+def mm(left, right):
+    return jnp.dot(left, right, preferred_element_type=jnp.float32)
+
+
+def mm_nt(left, right):
+    return lax.dot_general(
+        left, right, (((1,), (1,)), ((), ())), preferred_element_type=jnp.float32
+    )
+
+
+def mm_tn(left, right):
+    return lax.dot_general(
+        left, right, (((0,), (0,)), ((), ())), preferred_element_type=jnp.float32
+    )
+
+
+def low(values):
+    return values.astype(jnp.bfloat16)
+
+
+def lanes_below(rows, period, limit):
+    lane = lax.broadcasted_iota(jnp.int32, (rows, WIDE), 1)
+    return lane % period < limit
+
+
+def swap_halves(tile):
+    ahead = pltpu.roll(tile, WIDE - HEAD // 2, 1)
+    behind = pltpu.roll(tile, HEAD // 2, 1)
+    return jnp.where(lanes_below(tile.shape[0], HEAD, HEAD // 2), ahead, behind)
+
+
+def rope_tables(length):
+    half_width = HEAD // 2
+    freqs = jnp.exp(
+        jnp.arange(half_width, dtype=jnp.float32) * (-2.0 * math.log(rope_base) / HEAD)
+    )
+    angles = jnp.arange(length, dtype=jnp.float32)[:, None] * freqs[None, :]
+    cosines, sines = jnp.cos(angles), jnp.sin(angles)
+    return (
+        jnp.concatenate([cosines] * 4, axis=1),
+        jnp.concatenate([-sines, sines] * 2, axis=1),
+    )
+
+
+def project_body(x_ref, gain_ref, w_ref, cos_ref, sin_ref, normed_ref, qkv_ref):
+    values = x_ref[...].astype(jnp.float32)
+    inverse = lax.rsqrt(jnp.mean(values * values, axis=-1, keepdims=True) + epsilon)
+    normed = low(values * inverse * gain_ref[...])
+    normed_ref[...] = normed
+    cosines, sines = cos_ref[...], sin_ref[...]
+    width = qkv_ref.shape[1]
+    q_width, k_width = HEADS * HEAD, KV_HEADS * HEAD
+    step = 384
+    for at in range(0, width, step):
+        wide = mm(normed, w_ref[:, at : at + step])
+        for part in range(0, step, WIDE):
+            tile = wide[:, part : part + WIDE]
+            if at + part < q_width + k_width:
+                tile = tile * cosines + swap_halves(tile) * sines
+            if at + part < q_width:
+                tile = tile * HEAD ** (-0.5)
+            qkv_ref[:, at + part : at + part + WIDE] = low(tile)
+
+
+def project(x, gain, w, cosines, sines):
+    length, width = x.shape
+    out = w.shape[1]
+    rows = pl.BlockSpec((BLOCK, width), lambda i: (i, 0))
+    table = pl.BlockSpec((BLOCK, WIDE), lambda i: (i, 0))
+    return pl.pallas_call(
+        project_body,
+        grid=(length // BLOCK,),
+        in_specs=[
+            rows,
+            pl.BlockSpec((1, width), lambda i: (0, 0)),
+            pl.BlockSpec((width, out), lambda i: (0, 0), pipeline_mode=pl.Buffered(1)),
+            table,
+            table,
+        ],
+        out_specs=[rows, pl.BlockSpec((BLOCK, out), lambda i: (i, 0))],
+        out_shape=[
+            jax.ShapeDtypeStruct((length, width), jnp.bfloat16),
+            jax.ShapeDtypeStruct((length, out), jnp.bfloat16),
+        ],
+        cost_estimate=pl.CostEstimate(
+            flops=2 * length * width * out,
+            bytes_accessed=2 * (2 * length * width + length * out + width * out),
+            transcendentals=0,
+        ),
+        name="project",
+    )(x, gain, w, cosines, sines)
+
+
+def place_heads(tile, variants_ref):
+    wide = tile.astype(jnp.float32)
+    turned = pltpu.roll(wide, HEAD, 1)
+    low_lanes = lanes_below(tile.shape[0], WIDE, HEAD)
+    variants_ref[0] = low(jnp.where(low_lanes, wide, 0.0))
+    variants_ref[1] = low(jnp.where(low_lanes, 0.0, turned))
+    variants_ref[2] = low(jnp.where(low_lanes, turned, 0.0))
+    variants_ref[3] = low(jnp.where(low_lanes, 0.0, wide))
+
+
+def allowed_block(seg_k, seg_q, diagonal):
+    same = seg_k == seg_q
+    if diagonal:
+        rows = lax.broadcasted_iota(jnp.int32, same.shape, 0)
+        lanes = lax.broadcasted_iota(jnp.int32, same.shape, 1)
+        same = same & (rows <= lanes)
+    return same
+
+
+def attend_body(q_ref, k_ref, v_ref, seg_col_ref, seg_row_ref, mixed_ref, lse_ref, ks, vt, acc, stats):
+    block = pl.program_id(1)
+
+    @pl.when(block == 0)
+    def _():
+        place_heads(k_ref[...], ks)
+        vt[...] = low(v_ref[...].astype(jnp.float32).T)
+
+    acc[...] = jnp.zeros_like(acc)
+    stats[0] = jnp.full((8, BLOCK), -1e30, jnp.float32)
+    stats[1] = jnp.zeros((8, BLOCK), jnp.float32)
+    seg_q = seg_row_ref[...]
+
+    def step(j, diagonal):
+        rows = pl.ds(pl.multiple_of(j * BLOCK, BLOCK), BLOCK)
+        seg_k = seg_col_ref[rows, :]
+        allowed = allowed_block(seg_k, seg_q, diagonal)
+        for head in range(6):
+            part, side, kv = head // 2, head % 2, head // 3
+            q_tile = q_ref[:, part * WIDE : (part + 1) * WIDE]
+            scores = mm_nt(ks[kv * 2 + side, rows, :], q_tile)
+            scores = jnp.where(allowed, scores, -1e30)
+            before = stats[0, head : head + 1, :]
+            highest = jnp.maximum(before, jnp.max(scores, axis=0, keepdims=True))
+            shrink = jnp.exp(before - highest)
+            chances = jnp.exp(scores - highest)
+            stats[0, head : head + 1, :] = highest
+            stats[1, head : head + 1, :] = stats[1, head : head + 1, :] * shrink + jnp.sum(
+                chances, axis=0, keepdims=True
+            )
+            values = vt[kv * HEAD : (kv + 1) * HEAD, rows]
+            at = head * HEAD
+            acc[at : at + HEAD, :] = acc[at : at + HEAD, :] * shrink + mm(values, low(chances))
+
+    @pl.loop(0, block)
+    def _(j):
+        step(j, False)
+
+    step(block, True)
+    total = stats[1]
+    for part in range(3):
+        at = part * WIDE
+        both = jnp.concatenate(
+            [
+                acc[at : at + HEAD, :] / total[2 * part : 2 * part + 1, :],
+                acc[at + HEAD : at + WIDE, :] / total[2 * part + 1 : 2 * part + 2, :],
+            ],
+            axis=0,
+        )
+        mixed_ref[:, at : at + WIDE] = low(both.T)
+    lse_ref[0] = stats[0] + jnp.log(jnp.maximum(total, 1e-30))
+
+
+def attend(qkv, seg_col, seg_row):
+    length = qkv.shape[0]
+    pairs = KV_HEADS // 2
+    q_tiles = HEADS * HEAD // WIDE
+    return pl.pallas_call(
+        attend_body,
+        grid=(pairs, length // BLOCK),
+        in_specs=[
+            pl.BlockSpec((BLOCK, 3 * WIDE), lambda b, i: (i, b)),
+            pl.BlockSpec((length, WIDE), lambda b, i: (0, q_tiles + b)),
+            pl.BlockSpec((length, WIDE), lambda b, i: (0, q_tiles + pairs + b)),
+            pl.BlockSpec((length, 1), lambda b, i: (0, 0)),
+            pl.BlockSpec((1, BLOCK), lambda b, i: (0, i)),
+        ],
+        out_specs=[
+            pl.BlockSpec((BLOCK, 3 * WIDE), lambda b, i: (i, b)),
+            pl.BlockSpec((1, 8, BLOCK), lambda b, i: (b, 0, i)),
+        ],
+        out_shape=[
+            jax.ShapeDtypeStruct((length, HEADS * HEAD), jnp.bfloat16),
+            jax.ShapeDtypeStruct((pairs, 8, length), jnp.float32),
+        ],
+        scratch_shapes=[
+            pltpu.VMEM((4, length, WIDE), jnp.bfloat16),
+            pltpu.VMEM((WIDE, length), jnp.bfloat16),
+            pltpu.VMEM((6 * HEAD, BLOCK), jnp.float32),
+            pltpu.VMEM((2, 8, BLOCK), jnp.float32),
+        ],
+        cost_estimate=pl.CostEstimate(
+            flops=16 * length * length * HEADS * HEAD // 2,
+            bytes_accessed=6 * length * HEADS * HEAD,
+            transcendentals=HEADS * length * length // 2,
+        ),
+        name="attend",
+    )(qkv, qkv, qkv, seg_col, seg_row)
+
+
+def attend_back_body(
+    q_ref, k_ref, v_ref, grad_ref, mixed_ref, lse_ref, seg_col_ref, seg_row_ref, cos_ref, sin_ref,
+    dq_ref, dk_ref, dv_ref, ks, vs, kt, k_acc, v_acc, q_acc, sides, delta
+):
+    block = pl.program_id(1)
+    length = k_ref.shape[0]
+
+    @pl.when(block == 0)
+    def _():
+        place_heads(k_ref[...], ks)
+        place_heads(v_ref[...], vs)
+        kt[...] = low(k_ref[...].astype(jnp.float32).T)
+        k_acc[...] = jnp.zeros_like(k_acc)
+        v_acc[...] = jnp.zeros_like(v_acc)
+
+    q_acc[...] = jnp.zeros_like(q_acc)
+    seg_q = seg_row_ref[...]
+    low_lanes = lanes_below(BLOCK, WIDE, HEAD)
+    zero = jnp.zeros((BLOCK, WIDE), jnp.bfloat16)
+    for part in range(3):
+        at = part * WIDE
+        tile, grad = q_ref[:, at : at + WIDE], grad_ref[:, at : at + WIDE]
+        sides[0, part, 0:BLOCK, :] = jnp.where(low_lanes, tile, zero)
+        sides[0, part, BLOCK : 2 * BLOCK, :] = jnp.where(low_lanes, zero, tile)
+        sides[1, part, 0:BLOCK, :] = jnp.where(low_lanes, grad, zero)
+        sides[1, part, BLOCK : 2 * BLOCK, :] = jnp.where(low_lanes, zero, grad)
+        product = (grad.astype(jnp.float32) * mixed_ref[:, at : at + WIDE].astype(jnp.float32)).T
+        delta[2 * part : 2 * part + 1, :] = jnp.sum(product[:HEAD], axis=0, keepdims=True)
+        delta[2 * part + 1 : 2 * part + 2, :] = jnp.sum(product[HEAD:], axis=0, keepdims=True)
+
+    def step(j, diagonal):
+        rows = pl.ds(pl.multiple_of(j * BLOCK, BLOCK), BLOCK)
+        allowed = allowed_block(seg_col_ref[rows, :], seg_q, diagonal)
+        for part in range(3):
+            at = part * WIDE
+            q_tile, grad_tile = q_ref[:, at : at + WIDE], grad_ref[:, at : at + WIDE]
+            chances_pair, score_pair = [], []
+            for side in range(2):
+                head = 2 * part + side
+                kv = head // 3
+                scores = mm_nt(ks[kv * 2 + side, rows, :], q_tile)
+                scores = jnp.where(allowed, scores, -1e30)
+                chances = jnp.exp(scores - lse_ref[0, head : head + 1, :])
+                onto = mm_nt(vs[kv * 2 + side, rows, :], grad_tile)
+                score_grad = low(chances * (onto - delta[head : head + 1, :]))
+                chances_pair.append(low(chances))
+                score_pair.append(score_grad)
+                to = head * HEAD
+                q_acc[to : to + HEAD, :] += mm(kt[kv * HEAD : (kv + 1) * HEAD, rows], score_grad)
+            v_acc[part, rows, :] += mm(jnp.concatenate(chances_pair, axis=1), sides[1, part])
+            k_acc[part, rows, :] += mm(jnp.concatenate(score_pair, axis=1), sides[0, part])
+
+    @pl.loop(0, block)
+    def _(j):
+        step(j, False)
+
+    step(block, True)
+    here = pl.ds(pl.multiple_of(block * BLOCK, BLOCK), BLOCK)
+    for part in range(3):
+        at = part * WIDE
+        tile = q_acc[at : at + WIDE, :].T * HEAD ** (-0.5)
+        tile = tile * cos_ref[here, :] - swap_halves(tile) * sin_ref[here, :]
+        dq_ref[:, at : at + WIDE] = low(tile)
+
+    @pl.when(block == length // BLOCK - 1)
+    def _():
+        for j in range(0, length, BLOCK):
+            rows = slice(j, j + BLOCK)
+
+            def gather(acc):
+                first, middle, last = acc[0, rows, :], acc[1, rows, :], acc[2, rows, :]
+                return middle + jnp.where(
+                    low_lanes, first + pltpu.roll(first, HEAD, 1), last + pltpu.roll(last, HEAD, 1)
+                )
+
+            tile = gather(k_acc)
+            tile = tile * cos_ref[rows, :] - swap_halves(tile) * sin_ref[rows, :]
+            dk_ref[rows, :] = low(tile)
+            dv_ref[rows, :] = low(gather(v_acc))
+
+
+def attend_back(qkv, mixed_grad, mixed, lse, seg_col, seg_row, cosines, sines):
+    length = qkv.shape[0]
+    pairs = KV_HEADS // 2
+    q_tiles = HEADS * HEAD // WIDE
+    q_block = pl.BlockSpec((BLOCK, 3 * WIDE), lambda b, i: (i, b))
+    kv_block = pl.BlockSpec((length, WIDE), lambda b, i: (0, b))
+    table = pl.BlockSpec((length, WIDE), lambda b, i: (0, 0), pipeline_mode=pl.Buffered(1))
+    return pl.pallas_call(
+        attend_back_body,
+        grid=(pairs, length // BLOCK),
+        in_specs=[
+            q_block,
+            pl.BlockSpec((length, WIDE), lambda b, i: (0, q_tiles + b)),
+            pl.BlockSpec((length, WIDE), lambda b, i: (0, q_tiles + pairs + b)),
+            q_block,
+            q_block,
+            pl.BlockSpec((1, 8, BLOCK), lambda b, i: (b, 0, i)),
+            pl.BlockSpec((length, 1), lambda b, i: (0, 0)),
+            pl.BlockSpec((1, BLOCK), lambda b, i: (0, i)),
+            table,
+            table,
+        ],
+        out_specs=[q_block, kv_block, kv_block],
+        out_shape=[
+            jax.ShapeDtypeStruct((length, HEADS * HEAD), jnp.bfloat16),
+            jax.ShapeDtypeStruct((length, KV_HEADS * HEAD), jnp.bfloat16),
+            jax.ShapeDtypeStruct((length, KV_HEADS * HEAD), jnp.bfloat16),
+        ],
+        scratch_shapes=[
+            pltpu.VMEM((4, length, WIDE), jnp.bfloat16),
+            pltpu.VMEM((4, length, WIDE), jnp.bfloat16),
+            pltpu.VMEM((WIDE, length), jnp.bfloat16),
+            pltpu.VMEM((3, length, WIDE), jnp.float32),
+            pltpu.VMEM((3, length, WIDE), jnp.float32),
+            pltpu.VMEM((6 * HEAD, BLOCK), jnp.float32),
+            pltpu.VMEM((2, 3, 2 * BLOCK, WIDE), jnp.bfloat16),
+            pltpu.VMEM((8, BLOCK), jnp.float32),
+        ],
+        cost_estimate=pl.CostEstimate(
+            flops=40 * length * length * HEADS * HEAD // 2,
+            bytes_accessed=12 * length * HEADS * HEAD,
+            transcendentals=HEADS * length * length // 2,
+        ),
+        name="attend_back",
+    )(qkv, qkv, qkv, mixed_grad, mixed, lse, seg_col, seg_row, cosines, sines)
+
+
+def feed_body(which_ref, normed_ref, turned_ref, c_ref, gate_ref, up_ref, down_ref,
+              out_ref, back_ref, gate_grad_ref, up_grad_ref, down_grad_ref,
+              hidden_t, gate_low, up_low):
+    first = pl.program_id(0) == 0
+    length, width = normed_ref.shape
+
+    @pl.when(first)
+    def _():
+        out_ref[...] = jnp.zeros_like(out_ref)
+        back_ref[...] = jnp.zeros_like(back_ref)
+
+    for at in range(0, length, BLOCK):
+        rows = slice(at, at + BLOCK)
+        normed = normed_ref[rows, :]
+        gate_sum = mm(normed, gate_ref[...])
+        up_sum = mm(normed, up_ref[...])
+        hidden_grad = mm_nt(c_ref[rows, :], down_ref[...])
+        sigmoid = jax.nn.sigmoid(gate_sum)
+        activated = gate_sum * sigmoid
+        hidden = low(activated * up_sum)
+        gate_grad = low(hidden_grad * up_sum * (sigmoid + activated * (1.0 - sigmoid)))
+        up_grad = low(hidden_grad * activated)
+        hidden_t[:, rows] = hidden.T
+        gate_low[rows, :] = gate_grad
+        up_low[rows, :] = up_grad
+        out_ref[rows, :] += mm(hidden, down_ref[...])
+        back_ref[rows, :] += mm_nt(gate_grad, gate_ref[...]) + mm_nt(up_grad, up_ref[...])
+    step = 384
+    for at in range(0, width, step):
+        rows = slice(at, at + step)
+        gate_grad_ref[rows, :] = low(mm(turned_ref[rows, :], gate_low[...]))
+        up_grad_ref[rows, :] = low(mm(turned_ref[rows, :], up_low[...]))
+        down_grad_ref[:, rows] = low(mm(hidden_t[...], c_ref[:, rows]))
+
+
+def feed(which, normed, turned, c, gate, up, down):
+    length, width = normed.shape
+    wide = gate.shape[1] // 4
+    whole = pl.BlockSpec((length, width), lambda t, w: (0, 0), pipeline_mode=pl.Buffered(1))
+    columns = pl.BlockSpec((width, wide), lambda t, w: (0, w[0] + 2 * t))
+    rows = pl.BlockSpec((wide, width), lambda t, w: (w[0] + 2 * t, 0))
+    total = pl.BlockSpec((length, width), lambda t, w: (0, 0), pipeline_mode=pl.Buffered(1))
+    columns_out = pl.BlockSpec((width, wide), lambda t, w: (0, t))
+    return pl.pallas_call(
+        feed_body,
+        grid_spec=pltpu.PrefetchScalarGridSpec(
+            num_scalar_prefetch=1,
+            grid=(2,),
+            in_specs=[
+                whole,
+                pl.BlockSpec((width, length), lambda t, w: (0, 0), pipeline_mode=pl.Buffered(1)),
+                whole,
+                columns,
+                columns,
+                rows,
+            ],
+            out_specs=[
+                total,
+                total,
+                columns_out,
+                columns_out,
+                pl.BlockSpec((wide, width), lambda t, w: (t, 0)),
+            ],
+            scratch_shapes=[
+                pltpu.VMEM((wide, length), jnp.bfloat16),
+                pltpu.VMEM((length, wide), jnp.bfloat16),
+                pltpu.VMEM((length, wide), jnp.bfloat16),
+            ],
+        ),
+        out_shape=[
+            jax.ShapeDtypeStruct((length, width), jnp.float32),
+            jax.ShapeDtypeStruct((length, width), jnp.float32),
+            jax.ShapeDtypeStruct((width, 2 * wide), jnp.bfloat16),
+            jax.ShapeDtypeStruct((width, 2 * wide), jnp.bfloat16),
+            jax.ShapeDtypeStruct((2 * wide, width), jnp.bfloat16),
+        ],
+        compiler_params=pltpu.CompilerParams(vmem_limit_bytes=VMEM_MOST),
+        cost_estimate=pl.CostEstimate(
+            flops=18 * length * width * wide * 2,
+            bytes_accessed=12 * width * wide * 2 + 16 * length * width,
+            transcendentals=length * wide * 2,
+        ),
+        name="feed",
+    )(which, normed, turned, c, gate, up, down)
 
 
 def shortened(array):
@@ -66,7 +486,7 @@
     return inverse * (weighted - scaled * jnp.mean(weighted * scaled, axis=-1, keepdims=True))
 
 
-def local(
+def plain_local(
     inputs,
     segments,
     out_grad,
@@ -254,6 +674,225 @@
     )
 
 
+class Places:
+    def __init__(self, group_size):
+        self.group = lax.axis_index("group")
+        self.y = lax.axis_index("fsdp")
+        self.size = group_size
+        self.masks = {"core": 1, "x": 2, "zlo": 4, "zhi": 8}
+
+    def bit(self, name):
+        if name == "y":
+            return self.y
+        return (self.group // self.masks[name]) % 2
+
+    def swap(self, array, name):
+        if name == "y":
+            return lax.ppermute(array, "fsdp", [(0, 1), (1, 0)])
+        mask = self.masks[name]
+        return lax.ppermute(array, "group", [(i, i ^ mask) for i in range(self.size)])
+
+
+def part_of(array, axis, bit):
+    size = array.shape[axis] // 2
+    return lax.dynamic_slice_in_dim(array, bit * size, size, axis)
+
+
+def add_up(terms):
+    total = terms[0].astype(jnp.float32)
+    for term in terms[1:]:
+        total = total + term.astype(jnp.float32)
+    return low(total)
+
+
+def in_order(bit, own, other, axis):
+    return jnp.where(
+        bit == 0,
+        jnp.concatenate([own, other], axis=axis),
+        jnp.concatenate([other, own], axis=axis),
+    )
+
+
+def reduce_down(places, terms, stages):
+    for name, axis in stages:
+        bit = places.bit(name)
+        sent = add_up([part_of(term, axis, 1 - bit) for term in terms])
+        terms = [part_of(term, axis, bit) for term in terms] + [places.swap(sent, name)]
+    return add_up(terms)
+
+
+def gather_up(places, piece, stages):
+    for name, axis in stages:
+        piece = in_order(places.bit(name), piece, places.swap(piece, name), axis)
+    return piece
+
+
+def gather_rows(places, shard):
+    rows = shard.shape[0]
+    quarter = rows // 4
+    core, x = places.bit("core"), places.bit("x")
+    mine = x * 2 + core
+    first = places.swap(lax.dynamic_slice_in_dim(shard, mine * quarter, quarter, 0), "y")
+    second = places.swap(first, "x")
+    third = places.swap(first, "core")
+    fourth = places.swap(second, "core")
+    here = places.y * rows
+    there = (1 - places.y) * rows
+    full = jnp.zeros((2 * rows, shard.shape[1]), shard.dtype)
+    full = lax.dynamic_update_slice_in_dim(full, shard, here, 0)
+    for piece, index in ((first, mine), (second, mine ^ 2), (third, mine ^ 1), (fourth, mine ^ 3)):
+        full = lax.dynamic_update_slice_in_dim(full, piece, there + index * quarter, 0)
+    return full
+
+
+def norm_grad(grad, gain, scaled, inverse):
+    weighted = grad * gain
+    return inverse * (weighted - scaled * jnp.mean(weighted * scaled, axis=-1, keepdims=True))
+
+
+def paired_local(
+    group_size,
+    inputs,
+    segments,
+    out_grad,
+    attention_gain,
+    query_weight,
+    key_weight,
+    value_weight,
+    output_weight,
+    feedforward_gain,
+    gate_weight,
+    up_weight,
+    down_weight,
+):
+    places = Places(group_size)
+    y = places.y
+    span, length, width = inputs.shape[1], segments.shape[1], inputs.shape[2]
+    q_width = query_weight.shape[1]
+
+    def whole_sequence(blocks):
+        own = lax.dynamic_index_in_dim(blocks, y, 0, False)
+        other = places.swap(lax.dynamic_index_in_dim(blocks, 1 - y, 0, False), "y")
+        return in_order(y, own, other, 0)
+
+    def own_blocks(rows):
+        own = part_of(rows, 0, y)
+        other = places.swap(part_of(rows, 0, 1 - y), "y")
+        return in_order(y, own[None], other[None], 0)
+
+    gains = jnp.stack([attention_gain, feedforward_gain])
+    gains = in_order(y, gains, places.swap(gains, "y"), 1).astype(jnp.float32)
+    gain_a, gain_f = gains[0:1], gains[1:2]
+    tokens = whole_sequence(inputs)
+    qkv_weight = gather_rows(places, jnp.concatenate([query_weight, key_weight, value_weight], axis=1))
+    mix_weight = gather_rows(places, output_weight)
+    full_gate = gather_rows(places, gate_weight)
+    full_up = gather_rows(places, up_weight)
+    full_down = gather_rows(places, down_weight)
+    c = whole_sequence(out_grad)
+
+    segment = lax.dynamic_index_in_dim(segments, y, 0, False)
+    seg_col, seg_row = segment[:, None], segment[None, :]
+    cosines, sines = rope_tables(length)
+    normed_a, qkv = project(tokens, gain_a, qkv_weight, cosines, sines)
+    mixed, lse = attend(qkv, seg_col, seg_row)
+
+    values = tokens.astype(jnp.float32)
+    residual = values + mm(mixed, mix_weight)
+    inverse_f = lax.rsqrt(jnp.mean(residual * residual, axis=-1, keepdims=True) + epsilon)
+    normed_f = low(residual * inverse_f * gain_f)
+    turned_f = normed_f.T
+
+    core = places.bit("core")
+    theirs = feed((1 - core).reshape(1), normed_f, turned_f, c, full_gate, full_up, full_down)
+    mine = feed(core.reshape(1), normed_f, turned_f, c, full_gate, full_up, full_down)
+    result = low(residual + theirs[0] + mine[0])
+    outputs = own_blocks(result)
+
+    normed_f_grad = theirs[1] + mine[1]
+    scaled_f = residual * inverse_f
+    feed_gain_term = jnp.sum(normed_f_grad * scaled_f, axis=0)
+    residual_grad = c.astype(jnp.float32) + norm_grad(normed_f_grad, gain_f, scaled_f, inverse_f)
+    residual_low = low(residual_grad)
+    mix_term = low(mm_tn(mixed, residual_low))
+    mixed_grad = low(mm_nt(residual_low, mix_weight))
+
+    orders = (("y", "x", "zlo", "zhi"), ("x", "zlo", "y", "zhi"), ("zlo", "y", "x", "zhi"))
+    backs = (("zhi", "zlo", "x"), ("zhi", "x", "zlo"), ("zhi", "zlo", "x"))
+    dims = {"y": 0, "x": 1, "zlo": 2, "zhi": 3}
+    pieces = []
+    for index in range(3):
+        shape = mine[2 + index].shape
+        split = (2, 2, 2, shape[0] // 8, shape[1])
+        terms = [mine[2 + index].reshape(split), places.swap(theirs[2 + index], "core").reshape(split)]
+        piece = reduce_down(places, terms, [(name, dims[name]) for name in orders[index]])
+        pieces.append(gather_up(places, piece, [(name, dims[name]) for name in backs[index]]))
+
+    def hidden_columns(piece):
+        wide = piece.shape[-1] // 2
+        piece = piece.reshape(width // 2, 2, wide)
+        other = places.swap(piece, "core")
+        return in_order(core, piece[:, :, None], other[:, :, None], 2).reshape(width // 2, 4 * wide)
+
+    gate_sum_grad = hidden_columns(pieces[0]).astype(jnp.float32)
+    up_sum_grad = hidden_columns(pieces[1]).astype(jnp.float32)
+    down_piece = pieces[2].reshape(-1, width)
+    down_sum_grad = in_order(core, down_piece, places.swap(down_piece, "core"), 0).astype(jnp.float32)
+
+    dq, dk, dv = attend_back(qkv, mixed_grad, mixed, lse, seg_col, seg_row, cosines, sines)
+    lows = jnp.concatenate([dq, dk, dv], axis=1)
+    qkv_term = low(mm_tn(normed_a, lows))
+    normed_a_grad = mm_nt(lows, qkv_weight)
+    inverse_a = lax.rsqrt(jnp.mean(values * values, axis=-1, keepdims=True) + epsilon)
+    scaled_a = values * inverse_a
+    attention_gain_term = jnp.sum(normed_a_grad * scaled_a, axis=0)
+    token_grad = low(residual_grad + norm_grad(normed_a_grad, gain_a, scaled_a, inverse_a))
+    input_grads = own_blocks(token_grad)
+
+    dims = {"y": 0, "core": 1, "x": 2, "zlo": 3, "zhi": 4}
+
+    def whole_sum(term, order, back):
+        term = term.reshape(2, 2, 2, 2, term.shape[0] // 16, term.shape[1])
+        piece = reduce_down(places, [term], [(name, dims[name]) for name in order])
+        piece = gather_up(places, piece, [(name, dims[name]) for name in back])
+        return piece.reshape(-1, piece.shape[-1])
+
+    mix_sum_grad = whole_sum(
+        mix_term, ("core", "x", "y", "zlo", "zhi"), ("zhi", "zlo", "x", "core")
+    ).astype(jnp.float32)
+    third = qkv_term.shape[1] // 3
+    qkv_sum = jnp.concatenate(
+        [
+            whole_sum(
+                qkv_term[:, i * third : (i + 1) * third],
+                ("core",) + orders[i],
+                backs[i] + ("core",),
+            )
+            for i in range(3)
+        ],
+        axis=1,
+    ).astype(jnp.float32)
+
+    gain_terms = jnp.stack([attention_gain_term, feed_gain_term])
+    for name in ("core", "y", "x", "zlo", "zhi"):
+        gain_terms = gain_terms + places.swap(gain_terms, name)
+    gain_grads = part_of(gain_terms, 1, y)
+    k_width = key_weight.shape[1]
+    return (
+        outputs,
+        input_grads,
+        gain_grads[0],
+        qkv_sum[:, :q_width],
+        qkv_sum[:, q_width : q_width + k_width],
+        qkv_sum[:, q_width + k_width :],
+        mix_sum_grad,
+        gain_grads[1],
+        gate_sum_grad,
+        up_sum_grad,
+        down_sum_grad,
+    )
+
+
 def solution(mesh):
     placed = (
         P("group", "fsdp", None),
@@ -269,6 +908,13 @@
         P("fsdp", None),
         P("fsdp", None),
     )
+    group_size, fsdp_size = mesh.shape["group"], mesh.shape["fsdp"]
+
+    def local(*arrays):
+        if group_size == 16 and fsdp_size == 2 and arrays[0].shape[0] == 2:
+            return paired_local(group_size, *arrays)
+        return plain_local(*arrays)
+
     return jax.shard_map(
         local,
         mesh=mesh,

time: 2030 us -> 904 us (0.45)
  blocking collectives: 677 us -> 0 us
  matrix products: 564 us -> 34.6 us
  waiting for transfers between devices: 662 us -> 313 us
  Pallas kernels: 0 us -> 234 us
  local copies, waits for them, and re-layouts: 26.4 us -> 138 us
  starting transfers between devices: 0.67 us -> 94.3 us
    psum x1 -> x0, blocking collectives: 582 us -> none  [local(): summed = lax.psum(shards, 'group')]
    dot_general x52 -> x5, matrix products: 524 us -> 34.6 us  [the longest x2 14.8 us: mm_nt(): lax.dot_general(left, right, (((1,), (1,)), ((), ())), preferred_element_...]
    reduce_scatter x11 -> x0, waiting for transfers between devices: 345 us -> none  [the longest x7 345 us: local(): lax.psum_scatter(shortened(totals), 'fsdp', scatter_dimension=0, tiled=True)]
    all_gather x5 -> x0, waiting for transfers between devices: 314 us -> none  [the longest x1 90.8 us: local(): lax.all_gather(gate_weight, 'fsdp', axis=0, tiled=True)]
    ppermute x0 -> x93, waiting for transfers between devices: none -> 313 us  [the longest x75 192 us: swap(): lax.ppermute(array, 'group', [(i, i ^ mask) for i in range(self.size)])]
    pallas_call x0 -> x5, Pallas kernels: none -> 234 us  [the longest x2 91.8 us: feed(): pl.pallas_call(feed_body, grid_spec=pltpu.PrefetchScalarGridSpec(num_scal...]
    ppermute x0 -> x93, starting transfers between devices: none -> 94.3 us  [the longest x75 70.5 us: swap(): lax.ppermute(array, 'group', [(i, i ^ mask) for i in range(self.size)])]
    all_gather x6 -> x0, blocking collectives: 84.4 us -> none  [the longest x1 22.2 us: local(): lax.all_gather(value_weight, 'fsdp', axis=0, tiled=True)]
  transfers between devices with their start and end apart: 16 -> 93, of which waited for: 10 -> 45; matrix products, arithmetic and copies ran while one was open for 15% -> 22% of each run, Pallas kernels for 0% -> 8%
where the time goes in v1:
time: 904 us; the launch traced here: 896 us
  waiting for transfers between devices  313 us (35%)
  Pallas kernels  234 us (26%)
  local copies, waits for them, and re-layouts  138 us (15%)
  starting transfers between devices  94.3 us (10%)
  other arithmetic  80.9 us (9%)
  matrix products  34.6 us (4%)
    ppermute x75, waiting for transfers between devices, swap(): lax.ppermute(array, 'group', [(i, i ^ mask) for i in range(self.size)])  192 us
    ppermute x18, waiting for transfers between devices, swap(): return lax.ppermute(array, 'fsdp', [(0, 1), (1, 0)])  121 us
    pallas_call x2, Pallas kernels, feed(): pl.pallas_call(feed_body, grid_spec=pltpu.PrefetchScalarGridSpec(num_scal...  91.8 us
    ppermute x75, starting transfers between devices, swap(): lax.ppermute(array, 'group', [(i, i ^ mask) for i in range(self.size)])  70.5 us
    pallas_call x1, Pallas kernels, attend_back(): pl.pallas_call(attend_back_body, grid=(pairs, length // BLOCK), in_specs=...  69.5 us
    pallas_call x1, Pallas kernels, attend(): pl.pallas_call(attend_body, grid=(pairs, length // BLOCK), in_specs=[pl.B...  60.9 us
    dynamic_update_slice x20, local copies, waits for them, and re-layouts, gather_rows(): lax.dynamic_update_slice_in_dim(full, piece, there + index * quarter, 0)  27.3 us
    ppermute x18, starting transfers between devices, swap(): return lax.ppermute(array, 'fsdp', [(0, 1), (1, 0)])  23.8 us
  transfers between devices with their start and end apart: 93, of which 45 were waited for; matrix products, arithmetic and copies ran while one was open for 22% of the time, Pallas kernels for 8%

profile of v1, /device:TPU:0, one launch (start us, length us, event | category | flops | bytes accessed | tf_op | source)
XLA Modules:
  0.0 895.7 jit_solution(2327314389252295485)
XLA Ops:
  49.4 21.7 %collective-permute-done.1 = bf16[2,576]{1,0:T(2,128)(2,1)} collective-permute-done((bf16[2,576]{1,0:T(2,128)(2,1)}, bf16[2,576]{1,0:T(2,128)(2,1)}, u32[]{:S(2)}, u32[]{:S(2)}) %collective-permute-start.1) | collective-permute-done | bytes 2336 | tf_op jit(solution)/shard_map/ppermute | solution.py:691
  107.9 6.9 collective-permute-done
  118.9 20.8 %collective-permute-done.10 = bf16[512,1152]{1,0:T(8,128)(2,1)S(1)} collective-permute-done((bf16[512,1152]{1,0:T(8,128)(2,1)S(1)}, bf16[512,1152]{1,0:T(8,128)(2,1)S(1)}, u32[]{:S(2)}, u32[]{:S(2)}) %collective-permute-start.10) | collective-permute-done | bytes 1179680 | tf_op jit(solution)/shard_map/ppermute | solution.py:691
  144.5 11.4 %project.1 = (bf16[1024,1152]{1,0:T(8,128)(2,1)}, bf16[1024,1920]{1,0:T(8,128)(2,1)}) custom-call(bf16[1024,1152]{1,0:T(8,128)(2,1)} %get-tuple-element.54.x_ref, f32[1,1152]{1,0:T(1,128)} %get-tuple-element.78.gain_ref, bf16[1152,1920]{1,0:T(8,128)(2,1)} %constant_dynamic-update-slice_fusion.20.w_ref, f32[1024,128]{1,0:T(8,128)} %get-tuple-element.85.cos_ref, ...), custom_call_target="tpu_custom_call" | custom-call | flops 4529848320 | bytes 13074432 | tf_op jit(solution)/shard_map/project/pallas_call | solution.py:90
  155.9 60.9 %attend.1 = (bf16[1024,1152]{1,0:T(8,128)(2,1)}, f32[3,8,1024]{2,1,0:T(8,128)}) custom-call(bf16[1024,1920]{1,0:T(8,128)(2,1)} %get-tuple-element.28.q_ref.k_ref.v_ref, bf16[1024,1920]{1,0:T(8,128)(2,1)} %get-tuple-element.28.q_ref.k_ref.v_ref, bf16[1024,1920]{1,0:T(8,128)(2,1)} %get-tuple-element.28.q_ref.k_ref.v_ref, s32[1024,1]{1,0:T(8,128)} %copy.45.seg_col_ref, ...), custom_call_target="tpu_custom_call" | custom-call | flops 9663676416 | bytes 7077888 | tf_op jit(solution)/shard_map/attend/pallas_call | solution.py:190
  244.1 45.8 %feed.3 = (f32[1024,1152]{1,0:T(8,128)}, f32[1024,1152]{1,0:T(8,128)}, bf16[1152,1536]{1,0:T(8,128)(2,1)}, bf16[1152,1536]{1,0:T(8,128)(2,1)}, bf16[1536,1152]{1,0:T(8,128)(2,1)}) custom-call(s32[1]{0:T(128)} %bitcast.7.which_ref, bf16[1024,1152]{1,0:T(8,128)(2,1)} %multiply_convert_fusion.normed_ref, bf16[1152,1024]{1,0:T(8,128)(2,1)} %copy.46.turned_ref, ...), custom_call_target="tpu_custom_call" | custom-call | flops 32614907904 | bytes 40108032 | tf_op jit(solution)/shard_map/feed/pallas_call | solution.py:394
  290.0 46.0 %feed.2 = (f32[1024,1152]{1,0:T(8,128)}, f32[1024,1152]{1,0:T(8,128)}, bf16[1152,1536]{1,0:T(8,128)(2,1)}, bf16[1152,1536]{1,0:T(8,128)(2,1)}, bf16[1536,1152]{1,0:T(8,128)(2,1)}) custom-call(s32[1]{0:T(128)} %bitcast.3.which_ref, bf16[1024,1152]{1,0:T(8,128)(2,1)} %multiply_convert_fusion.normed_ref, bf16[1152,1024]{1,0:T(8,128)(2,1)} %copy.46.turned_ref, ...), custom_call_target="tpu_custom_call" | custom-call | flops 32614907904 | bytes 40108032 | tf_op jit(solution)/shard_map/feed/pallas_call | solution.py:394
  350.9 8.2 convolution_convert_fusion.1
  365.7 69.5 %attend_back.1 = (bf16[1024,1152]{1,0:T(8,128)(2,1)}, bf16[1024,384]{1,0:T(8,128)(2,1)}, bf16[1024,384]{1,0:T(8,128)(2,1)}) custom-call(bf16[1024,1920]{1,0:T(8,128)(2,1)} %get-tuple-element.28.q_ref.k_ref.v_ref, bf16[1024,1920]{1,0:T(8,128)(2,1)} %get-tuple-element.28.q_ref.k_ref.v_ref, bf16[1024,1920]{1,0:T(8,128)(2,1)} %get-tuple-element.28.q_ref.k_ref.v_ref, ...), custom_call_target="tpu_custom_call" | custom-call | flops 24159191040 | bytes 14155776 | tf_op jit(solution)/shard_map/attend_back/pallas_call | solution.py:311
  449.7 8.2 fusion.8
  479.3 44.8 %collective-permute-done.31 = bf16[1,1,2,2,72,640]{5,4,3,2,1,0:T(8,128)(2,1)S(1)} collective-permute-done((bf16[1,1,2,2,72,640]{5,4,3,2,1,0:T(8,128)(2,1)S(1)}, bf16[1,1,2,2,72,640]{5,4,3,2,1,0:T(8,128)(2,1)S(1)}, u32[]{:S(2)}, u32[]{:S(2)}) %collective-permute-start.31) | collective-permute-done | bytes 368672 | tf_op jit(solution)/shard_map/ppermute | solution.py:691
  623.2 33.4 %collective-permute-done.61 = bf16[1,1,1,1,36,1152]{5,4,3,2,1,0:T(8,128)(2,1)S(1)} collective-permute-done((bf16[1,1,1,1,36,1152]{5,4,3,2,1,0:T(8,128)(2,1)S(1)}, bf16[1,1,1,1,36,1152]{5,4,3,2,1,0:T(8,128)(2,1)S(1)}, u32[]{:S(2)}, u32[]{:S(2)}) %collective-permute-start.61) | collective-permute-done | bytes 82976 | tf_op jit(solution)/shard_map/ppermute | solution.py:693
  671.3 14.6 %collective-permute-done.86 = bf16[1,2,1,192,1152]{4,3,2,1,0:T(8,128)(2,1)S(1)} collective-permute-done((bf16[1,2,1,192,1152]{4,3,2,1,0:T(8,128)(2,1)S(1)}, bf16[1,2,1,192,1152]{4,3,2,1,0:T(8,128)(2,1)S(1)}, u32[]{:S(2)}, u32[]{:S(2)}) %collective-permute-start.86) | collective-permute-done | bytes 884768 | tf_op jit(solution)/shard_map/ppermute | solution.py:691
  693.4 11.1 %collective-permute-done.87 = bf16[1,1,1,192,1152]{4,3,2,1,0:T(8,128)(2,1)S(1)} collective-permute-done((bf16[1,1,1,192,1152]{4,3,2,1,0:T(8,128)(2,1)S(1)}, bf16[1,1,1,192,1152]{4,3,2,1,0:T(8,128)(2,1)S(1)}, u32[]{:S(2)}, u32[]{:S(2)}) %collective-permute-start.87) | collective-permute-done | bytes 442400 | tf_op jit(solution)/shard_map/ppermute | solution.py:693
  711.3 15.1 %collective-permute-done.88 = bf16[1,1,1,96,1152]{4,3,2,1,0:T(8,128)(2,1)S(1)} collective-permute-done((bf16[1,1,1,96,1152]{4,3,2,1,0:T(8,128)(2,1)S(1)}, bf16[1,1,1,96,1152]{4,3,2,1,0:T(8,128)(2,1)S(1)}, u32[]{:S(2)}, u32[]{:S(2)}) %collective-permute-start.88) | collective-permute-done | bytes 221216 | tf_op jit(solution)/shard_map/ppermute | solution.py:693
  726.8 9.1 %collective-permute-done.79 = bf16[1,1,1,72,1536]{4,3,2,1,0:T(8,128)(2,1)S(1)} collective-permute-done((bf16[1,1,1,72,1536]{4,3,2,1,0:T(8,128)(2,1)S(1)}, bf16[1,1,1,72,1536]{4,3,2,1,0:T(8,128)(2,1)S(1)}, u32[]{:S(2)}, u32[]{:S(2)}) %collective-permute-start.79) | collective-permute-done | bytes 221216 | tf_op jit(solution)/shard_map/ppermute | solution.py:693
  741.0 9.1 %collective-permute-done.89 = bf16[1,1,1,96,1152]{4,3,2,1,0:T(8,128)(2,1)S(1)} collective-permute-done((bf16[1,1,1,96,1152]{4,3,2,1,0:T(8,128)(2,1)S(1)}, bf16[1,1,1,96,1152]{4,3,2,1,0:T(8,128)(2,1)S(1)}, u32[]{:S(2)}, u32[]{:S(2)}) %collective-permute-start.89) | collective-permute-done | bytes 221216 | tf_op jit(solution)/shard_map/ppermute | solution.py:693
  771.8 8.2 collective-permute-done.72
  784.4 13.7 %collective-permute-done.82 = bf16[1,2,1,144,1536]{4,3,2,1,0:T(8,128)(2,1)S(1)} collective-permute-done((bf16[1,2,1,144,1536]{4,3,2,1,0:T(8,128)(2,1)S(1)}, bf16[1,2,1,144,1536]{4,3,2,1,0:T(8,128)(2,1)S(1)}, u32[]{:S(2)}, u32[]{:S(2)}) %collective-permute-start.82) | collective-permute-done | bytes 884768 | tf_op jit(solution)/shard_map/ppermute | solution.py:693
  807.1 12.2 %collective-permute-done.91 = bf16[1,1,2,192,1152]{4,3,2,1,0:T(8,128)(2,1)} collective-permute-done((bf16[1,1,2,192,1152]{4,3,2,1,0:T(8,128)(2,1)}, bf16[1,1,2,192,1152]{4,3,2,1,0:T(8,128)(2,1)}, u32[]{:S(2)}, u32[]{:S(2)}) %collective-permute-start.91) | collective-permute-done | bytes 884768 | tf_op jit(solution)/shard_map/ppermute | solution.py:693
  840.7 11.4 %copy.56 = f32[576,2,2,768]{3,2,1,0:T(2,128)} copy(f32[576,2,2,768]{3,0,2,1:T(8,128)} %fusion.11) | data formatting | bytes 14155776 | tf_op jit(solution)/shard_map/convert_element_type | solution.py:838
  852.1 10.0 %reshape.3154 = f32[576,3072]{1,0:T(8,128)} reshape(f32[576,2,2,768]{3,2,1,0:T(2,128)} %copy.56) | data formatting | bytes 14155776 | tf_op jit(solution)/shard_map/convert_element_type | solution.py:838
  867.4 11.4 %copy.52 = f32[576,2,2,768]{3,2,1,0:T(2,128)} copy(f32[576,2,2,768]{3,0,2,1:T(8,128)} %fusion.10) | data formatting | bytes 14155776 | tf_op jit(solution)/shard_map/convert_element_type | solution.py:837
  878.7 10.0 %reshape.3153 = f32[576,3072]{1,0:T(8,128)} reshape(f32[576,2,2,768]{3,2,1,0:T(2,128)} %copy.52) | data formatting | bytes 14155776 | tf_op jit(solution)/shard_map/convert_element_type | solution.py:837
  (439 shorter events, 380.1 us)
Async XLA Ops:
  3.0 92.1 %collective-permute-start.19 = (bf16[384,1152]{1,0:T(8,128)(2,1)}, bf16[384,1152]{1,0:T(8,128)(2,1)}, u32[]{:S(2)}, u32[]{:S(2)}) collective-permute-start(bf16[384,1152]{1,0:T(8,128)(2,1)} %constant_dynamic-slice_fusion.8), channel_id=1, source_target_pairs={{0,1},{1,0},{2,3},{3,2},{4,5},{5,4},{6,7},{7,6},{8,9},{9,8},{10,11... | collective-permute-start | bytes 2654216 | tf_op jit(solution)/shard_map/ppermute | solution.py:691
  8.2 81.2 %collective-permute-start.11 = (bf16[144,3072]{1,0:T(8,128)(2,1)}, bf16[144,3072]{1,0:T(8,128)(2,1)}, u32[]{:S(2)}, u32[]{:S(2)}) collective-permute-start(bf16[144,3072]{1,0:T(8,128)(2,1)} %constant_dynamic-slice_fusion.10), channel_id=1, source_target_pairs={{0,1},{1,0},{2,3},{3,2},{4,5},{5,4},{6,7},{7,6},{8,9},{9,8},{10,11... | collective-permute-start | bytes 2654216 | tf_op jit(solution)/shard_map/ppermute | solution.py:691
  9.1 83.8 %collective-permute-start.15 = (bf16[144,3072]{1,0:T(8,128)(2,1)}, bf16[144,3072]{1,0:T(8,128)(2,1)}, u32[]{:S(2)}, u32[]{:S(2)}) collective-permute-start(bf16[144,3072]{1,0:T(8,128)(2,1)} %constant_dynamic-slice_fusion.9), channel_id=1, source_target_pairs={{0,1},{1,0},{2,3},{3,2},{4,5},{5,4},{6,7},{7,6},{8,9},{9,8},{10,11... | collective-permute-start | bytes 2654216 | tf_op jit(solution)/shard_map/ppermute | solution.py:691
  12.9 62.0 %collective-permute-start.6 = (bf16[144,1152]{1,0:T(8,128)(2,1)}, bf16[144,1152]{1,0:T(8,128)(2,1)}, u32[]{:S(2)}, u32[]{:S(2)}) collective-permute-start(bf16[144,1152]{1,0:T(8,128)(2,1)} %constant_dynamic-slice_fusion.11), channel_id=1, source_target_pairs={{0,1},{1,0},{2,3},{3,2},{4,5},{5,4},{6,7},{7,6},{8,9},{9,8},{10,11... | collective-permute-start | bytes 995336 | tf_op jit(solution)/shard_map/ppermute | solution.py:691
  14.2 56.9 %collective-permute-start.1 = (bf16[2,576]{1,0:T(2,128)(2,1)}, bf16[2,576]{1,0:T(2,128)(2,1)}, u32[]{:S(2)}, u32[]{:S(2)}) collective-permute-start(bf16[2,576]{1,0:T(2,128)(2,1)} %pad_maximum_fusion.3), channel_id=1, source_target_pairs={{0,1},{1,0},{2,3},{3,2},{4,5},{5,4},{6,7},{7,6},{8,9},{9,8},{10,11... | collective-permute-start | bytes 6920 | tf_op jit(solution)/shard_map/ppermute | solution.py:691
  88.1 51.6 %collective-permute-start.10 = (bf16[512,1152]{1,0:T(8,128)(2,1)S(1)}, bf16[512,1152]{1,0:T(8,128)(2,1)S(1)}, u32[]{:S(2)}, u32[]{:S(2)}) collective-permute-start(bf16[512,1152]{1,0:T(8,128)(2,1)S(1)} %copy-done.26), channel_id=1, source_target_pairs={{0,1},{1,0},{2,3},{3,2},{4,5},{5,4},{6,7},{7,6},{8,9},{9,8},{10,11... | collective-permute-start | bytes 3538952 | tf_op jit(solution)/shard_map/ppermute | solution.py:691
  97.8 135.5 %collective-permute-start.20 = (bf16[384,1152]{1,0:T(8,128)(2,1)}, bf16[384,1152]{1,0:T(8,128)(2,1)}, u32[]{:S(2)}, u32[]{:S(2)}) collective-permute-start(bf16[384,1152]{1,0:T(8,128)(2,1)} %collective-permute-done.19), channel_id=1, source_target_pairs={{0,4},{2,6},{4,0},{6,2},{8,12},{10,14},{12,8},{14,10},{16,20},{18,... | collective-permute-start | bytes 2654216 | tf_op jit(solution)/shard_map/ppermute | solution.py:693
  104.8 134.3 %collective-permute-start.21 = (bf16[384,1152]{1,0:T(8,128)(2,1)}, bf16[384,1152]{1,0:T(8,128)(2,1)}, u32[]{:S(2)}, u32[]{:S(2)}) collective-permute-start(bf16[384,1152]{1,0:T(8,128)(2,1)} %collective-permute-done.19), channel_id=1, source_target_pairs={{0,2},{2,0},{4,6},{6,4},{8,10},{10,8},{12,14},{14,12},{16,18},{18,... | collective-permute-start | bytes 2654216 | tf_op jit(solution)/shard_map/ppermute | solution.py:693
  105.7 124.0 %collective-permute-start.12 = (bf16[144,3072]{1,0:T(8,128)(2,1)}, bf16[144,3072]{1,0:T(8,128)(2,1)}, u32[]{:S(2)}, u32[]{:S(2)}) collective-permute-start(bf16[144,3072]{1,0:T(8,128)(2,1)} %collective-permute-done.11), channel_id=1, source_target_pairs={{0,4},{2,6},{4,0},{6,2},{8,12},{10,14},{12,8},{14,10},{16,20},{18,... | collective-permute-start | bytes 2654216 | tf_op jit(solution)/shard_map/ppermute | solution.py:693
  139.7 93.8 %collective-permute-start.13 = (bf16[144,3072]{1,0:T(8,128)(2,1)}, bf16[144,3072]{1,0:T(8,128)(2,1)}, u32[]{:S(2)}, u32[]{:S(2)}) collective-permute-start(bf16[144,3072]{1,0:T(8,128)(2,1)} %collective-permute-done.11), channel_id=1, source_target_pairs={{0,2},{2,0},{4,6},{6,4},{8,10},{10,8},{12,14},{14,12},{16,18},{18,... | collective-permute-start | bytes 2654216 | tf_op jit(solution)/shard_map/ppermute | solution.py:693
  142.1 89.9 %collective-permute-start.16 = (bf16[144,3072]{1,0:T(8,128)(2,1)}, bf16[144,3072]{1,0:T(8,128)(2,1)S(1)}, u32[]{:S(2)}, u32[]{:S(2)}) collective-permute-start(bf16[144,3072]{1,0:T(8,128)(2,1)} %collective-permute-done.15), channel_id=1, source_target_pairs={{0,4},{2,6},{4,0},{6,2},{8,12},{10,14},{12,8},{14,10},{16,20},{18,... | collective-permute-start | bytes 2654216 | tf_op jit(solution)/shard_map/ppermute | solution.py:693
  463.7 63.2 %collective-permute-start.24 = (bf16[512,1152]{1,0:T(8,128)(2,1)S(1)}, bf16[512,1152]{1,0:T(8,128)(2,1)S(1)}, u32[]{:S(2)}, u32[]{:S(2)}) collective-permute-start(bf16[512,1152]{1,0:T(8,128)(2,1)S(1)} %get-tuple-element.61), channel_id=1, source_target_pairs={{0,1},{1,0},{2,3},{3,2},{4,5},{5,4},{6,7},{7,6},{8,9},{9,8},{10,11... | collective-permute-start | bytes 3538952 | tf_op jit(solution)/shard_map/ppermute | solution.py:691
  470.4 59.9 %collective-permute-start.23 = (bf16[512,1152]{1,0:T(8,128)(2,1)S(1)}, bf16[512,1152]{1,0:T(8,128)(2,1)S(1)}, u32[]{:S(2)}, u32[]{:S(2)}) collective-permute-start(bf16[512,1152]{1,0:T(8,128)(2,1)S(1)} %get-tuple-element.63), channel_id=1, source_target_pairs={{0,1},{1,0},{2,3},{3,2},{4,5},{5,4},{6,7},{7,6},{8,9},{9,8},{10,11... | collective-permute-start | bytes 3538952 | tf_op jit(solution)/shard_map/ppermute | solution.py:691
  477.0 49.7 %collective-permute-start.49 = (bf16[2,1,2,1,72,640]{5,4,3,2,1,0:T(8,128)(2,1)S(1)}, bf16[2,1,2,1,72,640]{5,4,3,2,1,0:T(8,128)(2,1)S(1)}, u32[]{:S(2)}, u32[]{:S(2)}) collective-permute-start(bf16[2,1,2,1,72,640]{5,4,3,2,1,0:T(8,128)(2,1)S(1)} %add_convert_fusion.11), channel_id=1, source_target_pairs={{0,8},{2,10},{4,12},{6,14},{8,0},{10,2},{12,4},{14,6},{16,24},{18,... | collective-permute-start | bytes 1105928 | tf_op jit(solution)/shard_map/ppermute | solution.py:693
  524.1 87.6 %collective-permute-start.84 = (bf16[1536,1152]{1,0:T(8,128)(2,1)}, bf16[1536,1152]{1,0:T(8,128)(2,1)S(1)}, u32[]{:S(2)}, u32[]{:S(2)}) collective-permute-start(bf16[1536,1152]{1,0:T(8,128)(2,1)} %get-tuple-element.44), channel_id=1, source_target_pairs={{0,2},{2,0},{4,6},{6,4},{8,10},{10,8},{12,14},{14,12},{16,18},{18,... | collective-permute-start | bytes 10616840 | tf_op jit(solution)/shard_map/ppermute | solution.py:693
  526.7 86.2 %collective-permute-start.75 = (bf16[1152,1536]{1,0:T(8,128)(2,1)}, bf16[1152,1536]{1,0:T(8,128)(2,1)S(1)}, u32[]{:S(2)}, u32[]{:S(2)}) collective-permute-start(bf16[1152,1536]{1,0:T(8,128)(2,1)} %get-tuple-element.42), channel_id=1, source_target_pairs={{0,2},{2,0},{4,6},{6,4},{8,10},{10,8},{12,14},{14,12},{16,18},{18,... | collective-permute-start | bytes 10616840 | tf_op jit(solution)/shard_map/ppermute | solution.py:693
  537.1 78.0 %collective-permute-start.66 = (bf16[1152,1536]{1,0:T(8,128)(2,1)S(1)}, bf16[1152,1536]{1,0:T(8,128)(2,1)S(1)}, u32[]{:S(2)}, u32[]{:S(2)}) collective-permute-start(bf16[1152,1536]{1,0:T(8,128)(2,1)S(1)} %copy-done.37), channel_id=1, source_target_pairs={{0,2},{2,0},{4,6},{6,4},{8,10},{10,8},{12,14},{14,12},{16,18},{18,... | collective-permute-start | bytes 10616840 | tf_op jit(solution)/shard_map/ppermute | solution.py:693
  547.1 51.8 %collective-permute-start.58 = (bf16[2,1,1,2,72,1152]{5,4,3,2,1,0:T(8,128)(2,1)S(1)}, bf16[2,1,1,2,72,1152]{5,4,3,2,1,0:T(8,128)(2,1)S(1)}, u32[]{:S(2)}, u32[]{:S(2)}) collective-permute-start(bf16[2,1,1,2,72,1152]{5,4,3,2,1,0:T(8,128)(2,1)S(1)} %add_convert_fusion.7), channel_id=1, source_target_pairs={{0,4},{2,6},{4,0},{6,2},{8,12},{10,14},{12,8},{14,10},{16,20},{18,... | collective-permute-start | bytes 1990664 | tf_op jit(solution)/shard_map/ppermute | solution.py:693
  613.0 52.7 %collective-permute-start.85 = (bf16[2,2,1,192,1152]{4,3,2,1,0:T(8,128)(2,1)S(1)}, bf16[2,2,1,192,1152]{4,3,2,1,0:T(8,128)(2,1)S(1)}, u32[]{:S(2)}, u32[]{:S(2)}) collective-permute-start(bf16[2,2,1,192,1152]{4,3,2,1,0:T(8,128)(2,1)S(1)} %add_convert_fusion.1), channel_id=1, source_target_pairs={{0,8},{2,10},{4,12},{6,14},{8,0},{10,2},{12,4},{14,6},{16,24},{18,... | collective-permute-start | bytes 5308424 | tf_op jit(solution)/shard_map/ppermute | solution.py:693
  615.0 52.3 %collective-permute-start.76 = (bf16[2,1,2,144,1536]{4,3,2,1,0:T(8,128)(2,1)S(1)}, bf16[2,1,2,144,1536]{4,3,2,1,0:T(8,128)(2,1)S(1)}, u32[]{:S(2)}, u32[]{:S(2)}) collective-permute-start(bf16[2,1,2,144,1536]{4,3,2,1,0:T(8,128)(2,1)S(1)} %add_convert_fusion.2), channel_id=1, source_target_pairs={{0,4},{2,6},{4,0},{6,2},{8,12},{10,14},{12,8},{14,10},{16,20},{18,... | collective-permute-start | bytes 5308424 | tf_op jit(solution)/shard_map/ppermute | solution.py:693
  617.0 50.8 %collective-permute-start.67 = (bf16[1,2,2,144,1536]{4,3,2,1,0:T(8,128)(2,1)S(1)}, bf16[1,2,2,144,1536]{4,3,2,1,0:T(8,128)(2,1)S(1)}, u32[]{:S(2)}, u32[]{:S(2)}) collective-permute-start(bf16[1,2,2,144,1536]{4,3,2,1,0:T(8,128)(2,1)S(1)} %add_convert_fusion.3), channel_id=1, source_target_pairs={{0,1},{1,0},{2,3},{3,2},{4,5},{5,4},{6,7},{7,6},{8,9},{9,8},{10,11... | collective-permute-start | bytes 5308424 | tf_op jit(solution)/shard_map/ppermute | solution.py:691
  670.4 113.0 %collective-permute-start.64 = (bf16[1,1,1,2,72,1152]{5,4,3,2,1,0:T(8,128)(2,1)S(1)}, bf16[1,1,1,2,72,1152]{5,4,3,2,1,0:T(8,128)(2,1)S(1)}, u32[]{:S(2)}, u32[]{:S(2)}) collective-permute-start(bf16[1,1,1,2,72,1152]{5,4,3,2,1,0:T(8,128)(2,1)S(1)} %maximum_select_fusion.28), channel_id=1, source_target_pairs={{0,4},{2,6},{4,0},{6,2},{8,12},{10,14},{12,8},{14,10},{16,20},{18,... | collective-permute-start | bytes 995336 | tf_op jit(solution)/shard_map/ppermute | solution.py:693
  807.1 55.1 %collective-permute-start.74 = (bf16[576,2,768]{2,1,0:T(2,128)(2,1)}, bf16[576,2,768]{2,1,0:T(2,128)(2,1)}, u32[]{:S(2)}, u32[]{:S(2)}) collective-permute-start(bf16[576,2,768]{2,1,0:T(2,128)(2,1)} %select_n.1376), channel_id=1, source_target_pairs={{0,2},{2,0},{4,6},{6,4},{8,10},{10,8},{12,14},{14,12},{16,18},{18,... | collective-permute-start | bytes 5308424 | tf_op jit(solution)/shard_map/ppermute | solution.py:693
  822.9 65.8 %collective-permute-start.92 = (bf16[768,1152]{1,0:T(8,128)(2,1)}, bf16[768,1152]{1,0:T(8,128)(2,1)}, u32[]{:S(2)}, u32[]{:S(2)}) collective-permute-start(bf16[768,1152]{1,0:T(8,128)(2,1)} %bitcast.61), channel_id=1, source_target_pairs={{0,2},{2,0},{4,6},{6,4},{8,10},{10,8},{12,14},{14,12},{16,18},{18,... | collective-permute-start | bytes 5308424 | tf_op jit(solution)/shard_map/ppermute | solution.py:693
  (114 other events, 1486.4 us)

commit v2 on v1

--- a/solution.py
+++ b/solution.py
@@ -111,6 +111,156 @@
     )(x, gain, w, cosines, sines)
 
 
+MESH = pl.DeviceIdType.MESH
+MASKS = {"core": 1, "x": 2, "zlo": 4, "zhi": 8}
+
+
+def bit_of(name):
+    if name == "y":
+        return lax.axis_index("fsdp")
+    return (lax.axis_index("group") // MASKS[name]) % 2
+
+
+def peer_of(name):
+    if name == "y":
+        return {"fsdp": 1 - lax.axis_index("fsdp")}
+    return {"group": lax.axis_index("group") + MASKS[name] * (1 - 2 * bit_of(name))}
+
+
+def greet(names):
+    barrier = pltpu.get_barrier_semaphore()
+    for name in names:
+        pl.semaphore_signal(barrier, inc=1, device_id=peer_of(name), device_id_type=MESH)
+    pl.semaphore_wait(barrier, len(names))
+
+
+def across(source, target, sems, slot, name):
+    return pltpu.make_async_remote_copy(
+        src_ref=source,
+        dst_ref=target,
+        send_sem=sems.at[0, slot],
+        recv_sem=sems.at[1, slot],
+        device_id=peer_of(name),
+        device_id_type=MESH,
+    )
+
+
+class Spread:
+    def __init__(self, shard, full, order, sems, slot, columns=None):
+        self.shard, self.full, self.order, self.sems, self.slot = shard, full, order, sems, slot
+        self.columns = columns
+
+    def copy(self, stage):
+        y = lax.axis_index("fsdp")
+        index = 0
+        for at, name in enumerate(self.order):
+            index = index + bit_of(name) * 2**at
+        slot = self.slot + stage
+        where = (slice(None), slice(None)) if self.columns is None else (slice(None), self.columns)
+        if stage == 0:
+            return across(
+                self.shard.at[index], self.full.at[(y * 8 + index,) + where], self.sems, slot, "y"
+            )
+        count = 2 ** (stage - 1)
+        block = self.full.at[(pl.ds((1 - y) * 8 + index // count * count, count),) + where]
+        return across(block, block, self.sems, slot, self.order[stage - 1])
+
+    def advance(self, stage):
+        if stage >= 0:
+            self.copy(stage).wait_recv()
+        if stage < len(self.order):
+            self.copy(stage + 1).start()
+
+    def finish(self):
+        for stage in range(len(self.order) + 1):
+            self.copy(stage).wait_send()
+
+
+def fetch_body(inputs, query, key, value, gains, tokens, weight, both_gains,
+               held, held_weight, sems, near):
+    y = lax.axis_index("fsdp")
+    q_width, k_width = query.shape[2], key.shape[2]
+    places = (
+        slice(0, q_width),
+        slice(q_width, q_width + k_width),
+        slice(q_width + k_width, q_width + 2 * k_width),
+    )
+    shards = (query, key, value)
+    loads = [pltpu.make_async_copy(inputs.at[y], held, near.at[0])] + [
+        pltpu.make_async_copy(shard, held_weight.at[:, :, place], near.at[1 + at])
+        for at, (shard, place) in enumerate(zip(shards, places))
+    ]
+    for load in loads:
+        load.start()
+    greet(("y", "x", "zlo", "core"))
+    index = bit_of("x") + 2 * bit_of("zlo") + 4 * bit_of("core")
+    first = [
+        across(shard.at[index], weight.at[y * 8 + index, :, place], sems, at, "y")
+        for at, (shard, place) in enumerate(zip(shards, places))
+    ]
+    span = held.shape[0]
+    swap = across(
+        inputs.at[1 - y], tokens.at[pl.ds(pl.multiple_of(y * span, span), span)], sems, 3, "y"
+    )
+    gain_swap = across(gains, both_gains.at[y], sems, 4, "y")
+    for copy in first + [gain_swap, swap]:
+        copy.start()
+    for load in loads:
+        load.wait()
+    stores = [
+        pltpu.make_async_copy(
+            held, tokens.at[pl.ds(pl.multiple_of(y * span, span), span)], near.at[4]
+        ),
+        pltpu.make_async_copy(held_weight, weight.at[pl.ds(y * 8, 8)], near.at[5]),
+        pltpu.make_async_copy(gains, both_gains.at[y], near.at[6]),
+    ]
+    for store in stores:
+        store.start()
+    for copy in first:
+        copy.wait_recv()
+    later = []
+    for at, name in enumerate(("x", "zlo", "core")):
+        count = 2**at
+        block = weight.at[pl.ds((1 - y) * 8 + index // count * count, count)]
+        copy = across(block, block, sems, 5 + at, name)
+        copy.start()
+        copy.wait_recv()
+        later.append(copy)
+    swap.wait_recv()
+    gain_swap.wait_recv()
+    for copy in first + [gain_swap, swap] + later:
+        copy.wait_send()
+    for store in stores:
+        store.wait()
+
+
+def fetch(inputs, query, key, value, gains):
+    span, width = inputs.shape[1:]
+    total = query.shape[1] + 2 * key.shape[1]
+    eight = lambda shard: shard.reshape(8, shard.shape[0] // 8, shard.shape[1])
+    rows = query.shape[0] // 8
+    anywhere = pl.BlockSpec(memory_space=pl.ANY)
+    tokens, weight, both_gains = pl.pallas_call(
+        fetch_body,
+        in_specs=[anywhere] * 5,
+        out_specs=[anywhere] * 3,
+        out_shape=[
+            jax.ShapeDtypeStruct((2 * span, width), inputs.dtype),
+            jax.ShapeDtypeStruct((16, rows, total), query.dtype),
+            jax.ShapeDtypeStruct((2,) + gains.shape, gains.dtype),
+        ],
+        scratch_shapes=[
+            pltpu.VMEM((span, width), inputs.dtype),
+            pltpu.VMEM((8, rows, total), query.dtype),
+            pltpu.SemaphoreType.DMA((2, 8)),
+            pltpu.SemaphoreType.DMA((7,)),
+        ],
+        compiler_params=pltpu.CompilerParams(collective_id=1, has_side_effects=True),
+        name="fetch",
+    )(inputs, eight(query), eight(key), eight(value), gains)
+    return tokens, weight.reshape(16 * rows, total), both_gains
+
+
 def place_heads(tile, variants_ref):
     wide = tile.astype(jnp.float32)
     turned = pltpu.roll(wide, HEAD, 1)
@@ -130,8 +280,65 @@
     return same
 
 
-def attend_body(q_ref, k_ref, v_ref, seg_col_ref, seg_row_ref, mixed_ref, lse_ref, ks, vt, acc, stats):
+def attend_body(
+    q_ref, k_ref, v_ref, seg_col_ref, seg_row_ref, out_grad, mix_w, gate_w, up_w, down_w,
+    mixed_ref, lse_ref, whole_grad, mix_full, gate_full, up_full, down_full,
+    ks, vt, acc, stats, sems, near, held_mix, held_gate, held_up, held_down, held_grad
+):
     block = pl.program_id(1)
+    now = pl.program_id(0) * pl.num_programs(1) + block
+    most = pl.num_programs(0) * pl.num_programs(1) - 1
+    y = lax.axis_index("fsdp")
+    spreads = {
+        "mix": Spread(mix_w, mix_full, ("x", "zlo", "core"), sems, 0),
+        "gate": Spread(gate_w, gate_full, ("zlo", "x", "core"), sems, 4),
+        "up": Spread(up_w, up_full, ("x", "zlo", "core"), sems, 8),
+        "down": Spread(down_w, down_full, ("zlo", "x", "core"), sems, 12),
+    }
+    span = out_grad.shape[1]
+    mine = whole_grad.at[pl.ds(pl.multiple_of(y * span, span), span)]
+    grad_swap = across(out_grad.at[1 - y], mine, sems, 16, "y")
+    half = pl.ds(y * 8, 8)
+    own = (
+        (mix_w, held_mix, mix_full.at[half]),
+        (gate_w, held_gate, gate_full.at[half]),
+        (up_w, held_up, up_full.at[half]),
+        (down_w, held_down, down_full.at[half]),
+        (out_grad.at[y], held_grad, mine),
+    )
+    loads = [pltpu.make_async_copy(a, b, near.at[0, at]) for at, (a, b, _) in enumerate(own)]
+    stores = [pltpu.make_async_copy(b, c, near.at[1, at]) for at, (_, b, c) in enumerate(own)]
+    plan = {
+        1: (("mix", 0),),
+        2: (("mix", 1),),
+        3: (("gate", 0), ("mix", 2)),
+        5: (("up", 0), ("gate", 1)),
+        7: (("down", 0), ("up", 1)),
+        9: (("gate", 2), ("down", 1)),
+        10: (("up", 2),),
+    }
+
+    @pl.when(now == 0)
+    def _():
+        for load in loads:
+            load.start()
+        greet(("y", "x", "zlo", "core"))
+        for name in ("mix", "gate", "up", "down"):
+            spreads[name].advance(-1)
+        grad_swap.start()
+
+    @pl.when(now == 1)
+    def _():
+        for load, store in zip(loads, stores):
+            load.wait()
+            store.start()
+
+    for at, steps in plan.items():
+
+        @pl.when(now == at)
+        def _(steps=steps):
+            for name, stage in steps:
+                spreads[name].advance(stage)
 
     @pl.when(block == 0)
     def _():
@@ -182,12 +389,25 @@
         mixed_ref[:, at : at + WIDE] = low(both.T)
     lse_ref[0] = stats[0] + jnp.log(jnp.maximum(total, 1e-30))
 
-
-def attend(qkv, seg_col, seg_row):
+    @pl.when(now == most)
+    def _():
+        spreads["down"].advance(2)
+        for spread in spreads.values():
+            spread.advance(3)
+            spread.finish()
+        grad_swap.wait()
+        for store in stores:
+            store.wait()
+
+
+def attend(qkv, seg_col, seg_row, out_grad, mix_w, gate_w, up_w, down_w):
     length = qkv.shape[0]
     pairs = KV_HEADS // 2
     q_tiles = HEADS * HEAD // WIDE
-    return pl.pallas_call(
+    anywhere = pl.BlockSpec(memory_space=pl.ANY)
+    shards = [w.reshape(8, w.shape[0] // 8, w.shape[1]) for w in (mix_w, gate_w, up_w, down_w)]
+    fulls = [jax.ShapeDtypeStruct((16,) + w.shape[1:], w.dtype) for w in shards]
+    found = pl.pallas_call(
         attend_body,
         grid=(pairs, length // BLOCK),
         in_specs=[
@@ -196,28 +416,40 @@
             pl.BlockSpec((length, WIDE), lambda b, i: (0, q_tiles + pairs + b)),
             pl.BlockSpec((length, 1), lambda b, i: (0, 0)),
             pl.BlockSpec((1, BLOCK), lambda b, i: (0, i)),
-        ],
+        ]
+        + [anywhere] * 5,
         out_specs=[
             pl.BlockSpec((BLOCK, 3 * WIDE), lambda b, i: (i, b)),
             pl.BlockSpec((1, 8, BLOCK), lambda b, i: (b, 0, i)),
-        ],
+        ]
+        + [anywhere] * 5,
         out_shape=[
             jax.ShapeDtypeStruct((length, HEADS * HEAD), jnp.bfloat16),
             jax.ShapeDtypeStruct((pairs, 8, length), jnp.float32),
-        ],
+            jax.ShapeDtypeStruct((length, out_grad.shape[2]), out_grad.dtype),
+        ]
+        + fulls,
         scratch_shapes=[
             pltpu.VMEM((4, length, WIDE), jnp.bfloat16),
             pltpu.VMEM((WIDE, length), jnp.bfloat16),
             pltpu.VMEM((6 * HEAD, BLOCK), jnp.float32),
             pltpu.VMEM((2, 8, BLOCK), jnp.float32),
-        ],
+            pltpu.SemaphoreType.DMA((2, 17)),
+            pltpu.SemaphoreType.DMA((2, 5)),
+        ]
+        + [pltpu.VMEM(w.shape, w.dtype) for w in shards]
+        + [pltpu.VMEM(out_grad.shape[1:], out_grad.dtype)],
+        compiler_params=pltpu.CompilerParams(
+            collective_id=2, has_side_effects=True, vmem_limit_bytes=VMEM_MOST
+        ),
         cost_estimate=pl.CostEstimate(
             flops=16 * length * length * HEADS * HEAD // 2,
             bytes_accessed=6 * length * HEADS * HEAD,
             transcendentals=HEADS * length * length // 2,
         ),
         name="attend",
-    )(qkv, qkv, qkv, seg_col, seg_row)
+    )(qkv, qkv, qkv, seg_col, seg_row, out_grad, *shards)
+    return tuple(found[:3]) + tuple(w.reshape(-1, w.shape[2]) for w in found[3:])
 
 
 def attend_back_body(
@@ -727,24 +959,6 @@
     return piece
 
 
-def gather_rows(places, shard):
-    rows = shard.shape[0]
-    quarter = rows // 4
-    core, x = places.bit("core"), places.bit("x")
-    mine = x * 2 + core
-    first = places.swap(lax.dynamic_slice_in_dim(shard, mine * quarter, quarter, 0), "y")
-    second = places.swap(first, "x")
-    third = places.swap(first, "core")
-    fourth = places.swap(second, "core")
-    here = places.y * rows
-    there = (1 - places.y) * rows
-    full = jnp.zeros((2 * rows, shard.shape[1]), shard.dtype)
-    full = lax.dynamic_update_slice_in_dim(full, shard, here, 0)
-    for piece, index in ((first, mine), (second, mine ^ 2), (third, mine ^ 1), (fourth, mine ^ 3)):
-        full = lax.dynamic_update_slice_in_dim(full, piece, there + index * quarter, 0)
-    return full
-
-
 def norm_grad(grad, gain, scaled, inverse):
     weighted = grad * gain
     return inverse * (weighted - scaled * jnp.mean(weighted * scaled, axis=-1, keepdims=True))
@@ -770,32 +984,25 @@
     span, length, width = inputs.shape[1], segments.shape[1], inputs.shape[2]
     q_width = query_weight.shape[1]
 
-    def whole_sequence(blocks):
-        own = lax.dynamic_index_in_dim(blocks, y, 0, False)
-        other = places.swap(lax.dynamic_index_in_dim(blocks, 1 - y, 0, False), "y")
-        return in_order(y, own, other, 0)
-
     def own_blocks(rows):
         own = part_of(rows, 0, y)
         other = places.swap(part_of(rows, 0, 1 - y), "y")
         return in_order(y, own[None], other[None], 0)
 
-    gains = jnp.stack([attention_gain, feedforward_gain])
-    gains = in_order(y, gains, places.swap(gains, "y"), 1).astype(jnp.float32)
+    gains = jnp.pad(
+        jnp.stack([attention_gain, feedforward_gain]).astype(jnp.float32), ((0, 6), (0, 0))
+    )
+    tokens, qkv_weight, gains = fetch(inputs, query_weight, key_weight, value_weight, gains)
+    gains = gains.transpose(1, 0, 2).reshape(8, width)
     gain_a, gain_f = gains[0:1], gains[1:2]
-    tokens = whole_sequence(inputs)
-    qkv_weight = gather_rows(places, jnp.concatenate([query_weight, key_weight, value_weight], axis=1))
-    mix_weight = gather_rows(places, output_weight)
-    full_gate = gather_rows(places, gate_weight)
-    full_up = gather_rows(places, up_weight)
-    full_down = gather_rows(places, down_weight)
-    c = whole_sequence(out_grad)
 
     segment = lax.dynamic_index_in_dim(segments, y, 0, False)
     seg_col, seg_row = segment[:, None], segment[None, :]
     cosines, sines = rope_tables(length)
     normed_a, qkv = project(tokens, gain_a, qkv_weight, cosines, sines)
-    mixed, lse = attend(qkv, seg_col, seg_row)
+    mixed, lse, c, mix_weight, full_gate, full_up, full_down = attend(
+        qkv, seg_col, seg_row, out_grad, output_weight, gate_weight, up_weight, down_weight
+    )
 
     values = tokens.astype(jnp.float32)
     residual = values + mm(mixed, mix_weight)

time: 904 us -> 889 us (0.983)
  Pallas kernels: 234 us -> 296 us
  waiting for transfers between devices: 313 us -> 251 us
  starting transfers between devices: 94.3 us -> 55.5 us
  other arithmetic: 80.9 us -> 114 us
  local copies, waits for them, and re-layouts: 138 us -> 124 us
    ppermute x18 -> x10, waiting for transfers between devices: 121 us -> 59.3 us  [swap(): return lax.ppermute(array, 'fsdp', [(0, 1), (1, 0)])]
    pallas_call x0 -> x1, Pallas kernels: none -> 37.2 us  [fetch(): pl.pallas_call(fetch_body, in_specs=[anywhere] * 5, out_specs=[anywhere]...]
    pallas_call x0 -> x6, local copies, waits for them, and re-layouts: none -> 33.1 us  [the longest x4 24.4 us: feed(): pl.pallas_call(feed_body, grid_spec=pltpu.PrefetchScalarGridSpec(num_scal...]
    dynamic_update_slice x25 -> x0, local copies, waits for them, and re-layouts: 32.9 us -> none  [the longest x20 27.3 us: gather_rows(): lax.dynamic_update_slice_in_dim(full, piece, there + index * quarter, 0)]
    ppermute x75 -> x60, starting transfers between devices: 70.5 us -> 42 us  [swap(): lax.ppermute(array, 'group', [(i, i ^ mask) for i in range(self.size)])]
    convert_element_type x37, other arithmetic: 18.6 us -> 46.6 us  [low(): return values.astype(jnp.bfloat16)]
    pallas_call x1, Pallas kernels: 60.9 us -> 86.3 us  [attend(): pl.pallas_call(attend_body, grid=(pairs, length // BLOCK), in_specs=[pl.B...]
    ppermute x18 -> x10, starting transfers between devices: 23.8 us -> 13.4 us  [swap(): return lax.ppermute(array, 'fsdp', [(0, 1), (1, 0)])]
  transfers between devices with their start and end apart: 93 -> 70, of which waited for: 45 -> 37; matrix products, arithmetic and copies ran while one was open for 22% -> 19% of each run, Pallas kernels for 8% -> 0%
where the time goes in v2:
time: 889 us; the launch traced here: 878 us
  Pallas kernels  296 us (33%)
  waiting for transfers between devices  251 us (28%)
  local copies, waits for them, and re-layouts  124 us (14%)
  other arithmetic  114 us (13%)
  starting transfers between devices  55.5 us (6%)
  matrix products  35.8 us (4%)
    ppermute x60, waiting for transfers between devices, swap(): lax.ppermute(array, 'group', [(i, i ^ mask) for i in range(self.size)])  192 us
    pallas_call x2, Pallas kernels, feed(): pl.pallas_call(feed_body, grid_spec=pltpu.PrefetchScalarGridSpec(num_scal...  91.8 us
    pallas_call x1, Pallas kernels, attend(): pl.pallas_call(attend_body, grid=(pairs, length // BLOCK), in_specs=[pl.B...  86.3 us
    pallas_call x1, Pallas kernels, attend_back(): pl.pallas_call(attend_back_body, grid=(pairs, length // BLOCK), in_specs=...  69.4 us
    ppermute x10, waiting for transfers between devices, swap(): return lax.ppermute(array, 'fsdp', [(0, 1), (1, 0)])  59.3 us
    convert_element_type x37, other arithmetic, low(): return values.astype(jnp.bfloat16)  46.6 us
    ppermute x60, starting transfers between devices, swap(): lax.ppermute(array, 'group', [(i, i ^ mask) for i in range(self.size)])  42 us
    pallas_call x1, Pallas kernels, fetch(): pl.pallas_call(fetch_body, in_specs=[anywhere] * 5, out_specs=[anywhere]...  37.2 us
  transfers between devices with their start and end apart: 70, of which 37 were waited for; matrix products, arithmetic and copies ran while one was open for 19% of the time, Pallas kernels for 0%

profile of v2, /device:TPU:0, one launch (start us, length us, event | category | flops | bytes accessed | tf_op | source)
XLA Modules:
  0.0 877.7 jit_solution(11336373951722604525)
XLA Ops:
  5.9 37.2 %fetch.1 = (bf16[1024,1152]{1,0:T(8,128)(2,1)}, bf16[16,72,1920]{2,1,0:T(8,128)(2,1)}, f32[2,8,576]{2,1,0:T(8,128)}) custom-call(bf16[2,512,1152]{2,1,0:T(8,128)(2,1)} %inputs.1, bf16[8,72,1152]{2,1,0:T(8,128)(2,1)} %bitcast.167, bf16[8,72,384]{2,1,0:T(8,128)(2,1)} %bitcast.178, bf16[8,72,384]{2,1,0:T(8,128)(2,1)} %bitcast.179, f32[8,576]{1,0:T(8,128)} %fusion.36.gains), custom_call_target="tpu_custom_call" | custom-call | tf_op jit(solution)/shard_map/fetch/pallas_call | solution.py:243
  52.1 11.4 %project.1 = (bf16[1024,1152]{1,0:T(8,128)(2,1)}, bf16[1024,1920]{1,0:T(8,128)(2,1)}) custom-call(bf16[1024,1152]{1,0:T(8,128)(2,1)} %get-tuple-element.36.x_ref, f32[1,1152]{1,0:T(1,128)} %slice.35.gain_ref, bf16[1152,1920]{1,0:T(8,128)(2,1)} %bitcast.188, f32[1024,128]{1,0:T(8,128)} %get-tuple-element.138.cos_ref, f32[1024,128]{1,0:T(8,128)} %get-tuple-element.139.sin_ref), custom_call_target="tpu_custom_call" | custom-call | flops 4529848320 | bytes 13074432 | tf_op jit(solution)/shard_map/project/pallas_call | solution.py:90
  63.5 86.3 %attend.1 = (bf16[1024,1152]{1,0:T(8,128)(2,1)}, f32[3,8,1024]{2,1,0:T(8,128)}, bf16[1024,1152]{1,0:T(8,128)(2,1)}, bf16[16,72,1152]{2,1,0:T(8,128)(2,1)}, bf16[...) custom-call(bf16[1024,1920]{1,0:T(8,128)(2,1)} %get-tuple-element.39.q_ref.k_ref.v_ref, ...), custom_call_target="tpu_custom_call" | custom-call | flops 9663676416 | bytes 7077888 | tf_op jit(solution)/shard_map/attend/pallas_call | solution.py:410
  149.8 8.8 %multiply_reduce_fusion.2 = (f32[1024]{0:T(1024)S(1)}, f32[1024,1152]{0,1:T(8,128)}) fusion(bf16[1024,1152]{1,0:T(8,128)(2,1)} %get-tuple-element.40.mixed_ref, bf16[1152,1152]{1,0:T(8,128)(2,1)} %bitcast.200, bf16[1024,1152]{0,1:T(8,128)(2,1)} %copy.78), kind=kOutput, calls=%fused_computation.20 | convolution fusion | flops 2722626560 | bytes 12095488 | tf_op jit(solution)/shard_map/dot_general | solution.py:22
  170.3 45.9 %feed.3 = (f32[1024,1152]{1,0:T(8,128)}, f32[1024,1152]{1,0:T(8,128)}, bf16[1152,1536]{1,0:T(8,128)(2,1)}, bf16[1152,1536]{1,0:T(8,128)(2,1)}, bf16[1536,1152]{1,0:T(8,128)(2,1)}) custom-call(s32[1]{0:T(128)} %bitcast.16.which_ref, bf16[1024,1152]{1,0:T(8,128)(2,1)} %copy.81.normed_ref, bf16[1152,1024]{1,0:T(8,128)(2,1)} %fusion.49.turned_ref, ...), custom_call_target="tpu_custom_call" | custom-call | flops 32614907904 | bytes 40108032 | tf_op jit(solution)/shard_map/feed/pallas_call | solution.py:626
  216.2 45.9 %feed.2 = (f32[1024,1152]{1,0:T(8,128)}, f32[1024,1152]{1,0:T(8,128)}, bf16[1152,1536]{1,0:T(8,128)(2,1)}, bf16[1152,1536]{1,0:T(8,128)(2,1)}, bf16[1536,1152]{1,0:T(8,128)(2,1)}) custom-call(s32[1]{0:T(128)} %bitcast.11.which_ref, bf16[1024,1152]{1,0:T(8,128)(2,1)} %copy.81.normed_ref, bf16[1152,1024]{1,0:T(8,128)(2,1)} %fusion.49.turned_ref, ...), custom_call_target="tpu_custom_call" | custom-call | flops 32614907904 | bytes 40108032 | tf_op jit(solution)/shard_map/feed/pallas_call | solution.py:626
  293.0 11.3 %multiply_add_fusion = (f32[1024,1152]{0,1:T(8,128)S(1)}, bf16[1024,1152]{0,1:T(8,128)(2,1)}) fusion(bf16[1024,1152]{0,1:T(8,128)(2,1)S(1)} %copy-done.6, f32[1024,1152]{0,1:T(8,128)} %get-tuple-element.136, f32[1024]{0:T(1024)S(1)} %broadcast_multiply_fusion.1, f32[1152]{0:T(1024)S(1)} %mul.272, f32[1024]{0:T(1024)S(1)} %add_rsqrt_fusion.1, ...), kind=kLoop, calls=%fused_computation.16 | loop fusion | flops 12976128 | bytes 33042944 | tf_op jit(solution)/shard_map/add | solution.py:1022
  309.2 69.4 %attend_back.1 = (bf16[1024,1152]{1,0:T(8,128)(2,1)}, bf16[1024,384]{1,0:T(8,128)(2,1)}, bf16[1024,384]{1,0:T(8,128)(2,1)}) custom-call(bf16[1024,1920]{1,0:T(8,128)(2,1)} %get-tuple-element.39.q_ref.k_ref.v_ref, bf16[1024,1920]{1,0:T(8,128)(2,1)} %get-tuple-element.39.q_ref.k_ref.v_ref, bf16[1024,1920]{1,0:T(8,128)(2,1)} %get-tuple-element.39.q_ref.k_ref.v_ref, ...), custom_call_target="tpu_custom_call" | custom-call | flops 24159191040 | bytes 14155776 | tf_op jit(solution)/shard_map/attend_back/pallas_call | solution.py:543
  398.4 10.4 %fusion.8 = (f32[1152]{0:T(1024)S(1)}, f32[1024]{0:T(1024)S(1)}, f32[1024,1152]{0,1:T(8,128)}) fusion(bf16[1024,1152]{0,1:T(8,128)(2,1)S(1)} %copy-done.3, f32[1024]{0:T(1024)S(1)} %add_rsqrt_fusion, f32[1152]{0:T(1024)S(1)} %mul.284, bf16[1024,1920]{1,0:T(8,128)(2,1)} %copy-done.19, bf16[1152,1920]{1,0:T(8,128)(2,1)} %bitcast.189), kind=kOutput, calls=%fused_computation.13 | convolution fusion | flops 4538103808 | bytes 15451136 | tf_op jit(solution)/shard_map/dot_general | solution.py:26
  427.0 19.3 %collective-permute-done.3 = f32[2,1152]{1,0:T(2,128)S(1)} collective-permute-done((f32[2,1152]{1,0:T(2,128)S(1)}, f32[2,1152]{1,0:T(2,128)S(1)}, u32[]{:S(2)}, u32[]{:S(2)}) %collective-permute-start.3) | collective-permute-done | bytes 9248 | tf_op jit(solution)/shard_map/ppermute | solution.py:923
  467.2 21.3 %collective-permute-done.8 = bf16[1,1,2,2,72,640]{5,4,3,2,1,0:T(8,128)(2,1)S(1)} collective-permute-done((bf16[1,1,2,2,72,640]{5,4,3,2,1,0:T(8,128)(2,1)S(1)}, bf16[1,1,2,2,72,640]{5,4,3,2,1,0:T(8,128)(2,1)S(1)}, u32[]{:S(2)}, u32[]{:S(2)}) %collective-permute-start.8) | collective-permute-done | bytes 368672 | tf_op jit(solution)/shard_map/ppermute | solution.py:923
  599.8 31.5 %collective-permute-done.38 = bf16[1,1,1,1,36,1152]{5,4,3,2,1,0:T(8,128)(2,1)S(1)} collective-permute-done((bf16[1,1,1,1,36,1152]{5,4,3,2,1,0:T(8,128)(2,1)S(1)}, bf16[1,1,1,1,36,1152]{5,4,3,2,1,0:T(8,128)(2,1)S(1)}, u32[]{:S(2)}, u32[]{:S(2)}) %collective-permute-start.38) | collective-permute-done | bytes 82976 | tf_op jit(solution)/shard_map/ppermute | solution.py:925
  650.0 12.4 %collective-permute-done.63 = bf16[1,2,1,192,1152]{4,3,2,1,0:T(8,128)(2,1)S(1)} collective-permute-done((bf16[1,2,1,192,1152]{4,3,2,1,0:T(8,128)(2,1)S(1)}, bf16[1,2,1,192,1152]{4,3,2,1,0:T(8,128)(2,1)S(1)}, u32[]{:S(2)}, u32[]{:S(2)}) %collective-permute-start.63) | collective-permute-done | bytes 884768 | tf_op jit(solution)/shard_map/ppermute | solution.py:923
  670.6 12.8 %collective-permute-done.64 = bf16[1,1,1,192,1152]{4,3,2,1,0:T(8,128)(2,1)S(1)} collective-permute-done((bf16[1,1,1,192,1152]{4,3,2,1,0:T(8,128)(2,1)S(1)}, bf16[1,1,1,192,1152]{4,3,2,1,0:T(8,128)(2,1)S(1)}, u32[]{:S(2)}, u32[]{:S(2)}) %collective-permute-start.64) | collective-permute-done | bytes 442400 | tf_op jit(solution)/shard_map/ppermute | solution.py:925
  690.3 13.6 %collective-permute-done.65 = bf16[1,1,1,96,1152]{4,3,2,1,0:T(8,128)(2,1)S(1)} collective-permute-done((bf16[1,1,1,96,1152]{4,3,2,1,0:T(8,128)(2,1)S(1)}, bf16[1,1,1,96,1152]{4,3,2,1,0:T(8,128)(2,1)S(1)}, u32[]{:S(2)}, u32[]{:S(2)}) %collective-permute-start.65) | collective-permute-done | bytes 221216 | tf_op jit(solution)/shard_map/ppermute | solution.py:925
  705.2 10.5 %collective-permute-done.56 = bf16[1,1,1,72,1536]{4,3,2,1,0:T(8,128)(2,1)S(1)} collective-permute-done((bf16[1,1,1,72,1536]{4,3,2,1,0:T(8,128)(2,1)S(1)}, bf16[1,1,1,72,1536]{4,3,2,1,0:T(8,128)(2,1)S(1)}, u32[]{:S(2)}, u32[]{:S(2)}) %collective-permute-start.56) | collective-permute-done | bytes 221216 | tf_op jit(solution)/shard_map/ppermute | solution.py:925
  717.1 10.5 %collective-permute-done.47 = bf16[1,1,1,72,1536]{4,3,2,1,0:T(8,128)(2,1)S(1)} collective-permute-done((bf16[1,1,1,72,1536]{4,3,2,1,0:T(8,128)(2,1)S(1)}, bf16[1,1,1,72,1536]{4,3,2,1,0:T(8,128)(2,1)S(1)}, u32[]{:S(2)}, u32[]{:S(2)}) %collective-permute-start.47) | collective-permute-done | bytes 221216 | tf_op jit(solution)/shard_map/ppermute | solution.py:925
  749.8 10.9 %collective-permute-done.49 = bf16[1,1,1,144,1536]{4,3,2,1,0:T(8,128)(2,1)S(1)} collective-permute-done((bf16[1,1,1,144,1536]{4,3,2,1,0:T(8,128)(2,1)S(1)}, bf16[1,1,1,144,1536]{4,3,2,1,0:T(8,128)(2,1)S(1)}, u32[]{:S(2)}, u32[]{:S(2)}) %collective-permute-start.49) | collective-permute-done | bytes 442400 | tf_op jit(solution)/shard_map/ppermute | solution.py:925
  765.2 14.5 %collective-permute-done.59 = bf16[1,2,1,144,1536]{4,3,2,1,0:T(8,128)(2,1)S(1)} collective-permute-done((bf16[1,2,1,144,1536]{4,3,2,1,0:T(8,128)(2,1)S(1)}, bf16[1,2,1,144,1536]{4,3,2,1,0:T(8,128)(2,1)S(1)}, u32[]{:S(2)}, u32[]{:S(2)}) %collective-permute-start.59) | collective-permute-done | bytes 884768 | tf_op jit(solution)/shard_map/ppermute | solution.py:925
  787.8 13.7 %collective-permute-done.68 = bf16[1,1,2,192,1152]{4,3,2,1,0:T(8,128)(2,1)} collective-permute-done((bf16[1,1,2,192,1152]{4,3,2,1,0:T(8,128)(2,1)}, bf16[1,1,2,192,1152]{4,3,2,1,0:T(8,128)(2,1)}, u32[]{:S(2)}, u32[]{:S(2)}) %collective-permute-start.68) | collective-permute-done | bytes 884768 | tf_op jit(solution)/shard_map/ppermute | solution.py:925
  822.8 11.4 %copy.98 = f32[576,2,2,768]{3,2,1,0:T(2,128)} copy(f32[576,2,2,768]{3,0,2,1:T(8,128)} %fusion.11) | data formatting | bytes 14155776 | tf_op jit(solution)/shard_map/convert_element_type | solution.py:1045
  834.3 10.1 %reshape.3207 = f32[576,3072]{1,0:T(8,128)} reshape(f32[576,2,2,768]{3,2,1,0:T(2,128)} %copy.98) | data formatting | bytes 14155776 | tf_op jit(solution)/shard_map/convert_element_type | solution.py:1045
  849.4 11.3 %copy.94 = f32[576,2,2,768]{3,2,1,0:T(2,128)} copy(f32[576,2,2,768]{3,0,2,1:T(8,128)} %fusion.10) | data formatting | bytes 14155776 | tf_op jit(solution)/shard_map/convert_element_type | solution.py:1044
  860.7 10.0 %reshape.3206 = f32[576,3072]{1,0:T(8,128)} reshape(f32[576,2,2,768]{3,2,1,0:T(2,128)} %copy.94) | data formatting | bytes 14155776 | tf_op jit(solution)/shard_map/convert_element_type | solution.py:1044
  (334 shorter events, 335.6 us)
Async XLA Ops:
  392.8 64.5 %collective-permute-start.7 = (bf16[2,1,2,2,72,640]{5,4,3,2,1,0:T(8,128)(2,1)}, bf16[2,1,2,2,72,640]{5,4,3,2,1,0:T(8,128)(2,1)}, u32[]{:S(2)}, u32[]{:S(2)}) collective-permute-start(bf16[2,1,2,2,72,640]{5,4,3,2,1,0:T(8,128)(2,1)} %constant_dynamic-slice_fusion.4), channel_id=1, source_target_pairs={{0,2},{2,0},{4,6},{6,4},{8,10},{10,8},{12,14},{14,12},{16,18},{18,... | collective-permute-start | bytes 2211848 | tf_op jit(solution)/shard_map/ppermute | solution.py:925
  395.2 65.9 %collective-permute-start.16 = (bf16[2,1,2,2,72,640]{5,4,3,2,1,0:T(8,128)(2,1)}, bf16[2,1,2,2,72,640]{5,4,3,2,1,0:T(8,128)(2,1)}, u32[]{:S(2)}, u32[]{:S(2)}) collective-permute-start(bf16[2,1,2,2,72,640]{5,4,3,2,1,0:T(8,128)(2,1)} %constant_dynamic-slice_fusion.3), channel_id=1, source_target_pairs={{0,2},{2,0},{4,6},{6,4},{8,10},{10,8},{12,14},{14,12},{16,18},{18,... | collective-permute-start | bytes 2211848 | tf_op jit(solution)/shard_map/ppermute | solution.py:925
  397.4 65.8 %collective-permute-start.25 = (bf16[2,1,2,2,72,640]{5,4,3,2,1,0:T(8,128)(2,1)}, bf16[2,1,2,2,72,640]{5,4,3,2,1,0:T(8,128)(2,1)}, u32[]{:S(2)}, u32[]{:S(2)}) collective-permute-start(bf16[2,1,2,2,72,640]{5,4,3,2,1,0:T(8,128)(2,1)} %constant_dynamic-slice_fusion.1), channel_id=1, source_target_pairs={{0,2},{2,0},{4,6},{6,4},{8,10},{10,8},{12,14},{14,12},{16,18},{18,... | collective-permute-start | bytes 2211848 | tf_op jit(solution)/shard_map/ppermute | solution.py:925
  417.8 77.0 %collective-permute-start.1 = (bf16[512,1152]{0,1:T(8,128)(2,1)S(1)}, bf16[512,1152]{0,1:T(8,128)(2,1)S(1)}, u32[]{:S(2)}, u32[]{:S(2)}) collective-permute-start(bf16[512,1152]{0,1:T(8,128)(2,1)S(1)} %get-tuple-element.119), channel_id=1, source_target_pairs={{0,1},{1,0},{2,3},{3,2},{4,5},{5,4},{6,7},{7,6},{8,9},{9,8},{10,11... | collective-permute-start | bytes 3538952 | tf_op jit(solution)/shard_map/ppermute | solution.py:923
  455.3 42.6 %collective-permute-start = (bf16[512,1152]{0,1:T(8,128)(2,1)}, bf16[512,1152]{0,1:T(8,128)(2,1)S(1)}, u32[]{:S(2)}, u32[]{:S(2)}) collective-permute-start(bf16[512,1152]{0,1:T(8,128)(2,1)} %get-tuple-element.121), channel_id=1, source_target_pairs={{0,1},{1,0},{2,3},{3,2},{4,5},{5,4},{6,7},{7,6},{8,9},{9,8},{10,11... | collective-permute-start | bytes 3538952 | tf_op jit(solution)/shard_map/ppermute | solution.py:923
  488.5 98.3 %collective-permute-start.61 = (bf16[1536,1152]{1,0:T(8,128)(2,1)}, bf16[1536,1152]{1,0:T(8,128)(2,1)}, u32[]{:S(2)}, u32[]{:S(2)}) collective-permute-start(bf16[1536,1152]{1,0:T(8,128)(2,1)} %get-tuple-element.60), channel_id=1, source_target_pairs={{0,2},{2,0},{4,6},{6,4},{8,10},{10,8},{12,14},{14,12},{16,18},{18,... | collective-permute-start | bytes 10616840 | tf_op jit(solution)/shard_map/ppermute | solution.py:925
  492.6 96.4 %collective-permute-start.52 = (bf16[1152,1536]{1,0:T(8,128)(2,1)}, bf16[1152,1536]{1,0:T(8,128)(2,1)}, u32[]{:S(2)}, u32[]{:S(2)}) collective-permute-start(bf16[1152,1536]{1,0:T(8,128)(2,1)} %get-tuple-element.58), channel_id=1, source_target_pairs={{0,2},{2,0},{4,6},{6,4},{8,10},{10,8},{12,14},{14,12},{16,18},{18,... | collective-permute-start | bytes 10616840 | tf_op jit(solution)/shard_map/ppermute | solution.py:925
  510.3 82.9 %collective-permute-start.43 = (bf16[1152,1536]{1,0:T(8,128)(2,1)}, bf16[1152,1536]{1,0:T(8,128)(2,1)S(1)}, u32[]{:S(2)}, u32[]{:S(2)}) collective-permute-start(bf16[1152,1536]{1,0:T(8,128)(2,1)} %get-tuple-element.56), channel_id=1, source_target_pairs={{0,2},{2,0},{4,6},{6,4},{8,10},{10,8},{12,14},{14,12},{16,18},{18,... | collective-permute-start | bytes 10616840 | tf_op jit(solution)/shard_map/ppermute | solution.py:925
  521.2 50.8 %collective-permute-start.35 = (bf16[2,1,1,2,72,1152]{5,4,3,2,1,0:T(8,128)(2,1)S(1)}, bf16[2,1,1,2,72,1152]{5,4,3,2,1,0:T(8,128)(2,1)S(1)}, u32[]{:S(2)}, u32[]{:S(2)}) collective-permute-start(bf16[2,1,1,2,72,1152]{5,4,3,2,1,0:T(8,128)(2,1)S(1)} %add_convert_fusion.7), channel_id=1, source_target_pairs={{0,4},{2,6},{4,0},{6,2},{8,12},{10,14},{12,8},{14,10},{16,20},{18,... | collective-permute-start | bytes 1990664 | tf_op jit(solution)/shard_map/ppermute | solution.py:925
  589.0 52.2 %collective-permute-start.62 = (bf16[2,2,1,192,1152]{4,3,2,1,0:T(8,128)(2,1)S(1)}, bf16[2,2,1,192,1152]{4,3,2,1,0:T(8,128)(2,1)S(1)}, u32[]{:S(2)}, u32[]{:S(2)}) collective-permute-start(bf16[2,2,1,192,1152]{4,3,2,1,0:T(8,128)(2,1)S(1)} %add_convert_fusion.1), channel_id=1, source_target_pairs={{0,8},{2,10},{4,12},{6,14},{8,0},{10,2},{12,4},{14,6},{16,24},{18,... | collective-permute-start | bytes 5308424 | tf_op jit(solution)/shard_map/ppermute | solution.py:925
  593.2 50.5 %collective-permute-start.53 = (bf16[2,1,2,144,1536]{4,3,2,1,0:T(8,128)(2,1)S(1)}, bf16[2,1,2,144,1536]{4,3,2,1,0:T(8,128)(2,1)S(1)}, u32[]{:S(2)}, u32[]{:S(2)}) collective-permute-start(bf16[2,1,2,144,1536]{4,3,2,1,0:T(8,128)(2,1)S(1)} %add_convert_fusion.2), channel_id=1, source_target_pairs={{0,4},{2,6},{4,0},{6,2},{8,12},{10,14},{12,8},{14,10},{16,20},{18,... | collective-permute-start | bytes 5308424 | tf_op jit(solution)/shard_map/ppermute | solution.py:925
  594.7 52.6 %collective-permute-start.44 = (bf16[1,2,2,144,1536]{4,3,2,1,0:T(8,128)(2,1)S(1)}, bf16[1,2,2,144,1536]{4,3,2,1,0:T(8,128)(2,1)S(1)}, u32[]{:S(2)}, u32[]{:S(2)}) collective-permute-start(bf16[1,2,2,144,1536]{4,3,2,1,0:T(8,128)(2,1)S(1)} %add_convert_fusion.3), channel_id=1, source_target_pairs={{0,1},{1,0},{2,3},{3,2},{4,5},{5,4},{6,7},{7,6},{8,9},{9,8},{10,11... | collective-permute-start | bytes 5308424 | tf_op jit(solution)/shard_map/ppermute | solution.py:923
  597.2 38.6 %collective-permute-start.33 = (bf16[1,1,2,2,72,640]{5,4,3,2,1,0:T(8,128)(2,1)S(1)}, bf16[1,1,2,2,72,640]{5,4,3,2,1,0:T(8,128)(2,1)S(1)}, u32[]{:S(2)}, u32[]{:S(2)}) collective-permute-start(bf16[1,1,2,2,72,640]{5,4,3,2,1,0:T(8,128)(2,1)S(1)} %maximum_select_fusion.24), channel_id=1, source_target_pairs={{0,2},{2,0},{4,6},{6,4},{8,10},{10,8},{12,14},{14,12},{16,18},{18,... | collective-permute-start | bytes 1105928 | tf_op jit(solution)/shard_map/ppermute | solution.py:925
  598.3 33.0 %collective-permute-start.38 = (bf16[1,1,1,1,36,1152]{5,4,3,2,1,0:T(8,128)(2,1)S(1)}, bf16[1,1,1,1,36,1152]{5,4,3,2,1,0:T(8,128)(2,1)S(1)}, u32[]{:S(2)}, u32[]{:S(2)}) collective-permute-start(bf16[1,1,1,1,36,1152]{5,4,3,2,1,0:T(8,128)(2,1)S(1)} %add_convert_fusion.26), channel_id=1, source_target_pairs={{0,16},{2,18},{4,20},{6,22},{8,24},{10,26},{12,28},{14,30},{16,0},... | collective-permute-start | bytes 248840 | tf_op jit(solution)/shard_map/ppermute | solution.py:925
  647.9 116.3 %collective-permute-start.41 = (bf16[1,1,1,2,72,1152]{5,4,3,2,1,0:T(8,128)(2,1)S(1)}, bf16[1,1,1,2,72,1152]{5,4,3,2,1,0:T(8,128)(2,1)S(1)}, u32[]{:S(2)}, u32[]{:S(2)}) collective-permute-start(bf16[1,1,1,2,72,1152]{5,4,3,2,1,0:T(8,128)(2,1)S(1)} %maximum_select_fusion.26), channel_id=1, source_target_pairs={{0,4},{2,6},{4,0},{6,2},{8,12},{10,14},{12,8},{14,10},{16,20},{18,... | collective-permute-start | bytes 995336 | tf_op jit(solution)/shard_map/ppermute | solution.py:925
  687.0 28.8 %collective-permute-start.56 = (bf16[1,1,1,72,1536]{4,3,2,1,0:T(8,128)(2,1)S(1)}, bf16[1,1,1,72,1536]{4,3,2,1,0:T(8,128)(2,1)S(1)}, u32[]{:S(2)}, u32[]{:S(2)}) collective-permute-start(bf16[1,1,1,72,1536]{4,3,2,1,0:T(8,128)(2,1)S(1)} %add_convert_fusion.18), channel_id=1, source_target_pairs={{0,16},{2,18},{4,20},{6,22},{8,24},{10,26},{12,28},{14,30},{16,0},... | collective-permute-start | bytes 663560 | tf_op jit(solution)/shard_map/ppermute | solution.py:925
  689.1 38.5 %collective-permute-start.47 = (bf16[1,1,1,72,1536]{4,3,2,1,0:T(8,128)(2,1)S(1)}, bf16[1,1,1,72,1536]{4,3,2,1,0:T(8,128)(2,1)S(1)}, u32[]{:S(2)}, u32[]{:S(2)}) collective-permute-start(bf16[1,1,1,72,1536]{4,3,2,1,0:T(8,128)(2,1)S(1)} %add_convert_fusion.20), channel_id=1, source_target_pairs={{0,16},{2,18},{4,20},{6,22},{8,24},{10,26},{12,28},{14,30},{16,0},... | collective-permute-start | bytes 663560 | tf_op jit(solution)/shard_map/ppermute | solution.py:925
  732.4 28.9 %collective-permute-start.67 = (bf16[1,1,1,192,1152]{4,3,2,1,0:T(8,128)(2,1)S(1)}, bf16[1,1,1,192,1152]{4,3,2,1,0:T(8,128)(2,1)S(1)}, u32[]{:S(2)}, u32[]{:S(2)}) collective-permute-start(bf16[1,1,1,192,1152]{4,3,2,1,0:T(8,128)(2,1)S(1)} %maximum_select_fusion.21), channel_id=1, source_target_pairs={{0,8},{2,10},{4,12},{6,14},{8,0},{10,2},{12,4},{14,6},{16,24},{18,... | collective-permute-start | bytes 1327112 | tf_op jit(solution)/shard_map/ppermute | solution.py:925
  749.8 29.9 %collective-permute-start.59 = (bf16[1,2,1,144,1536]{4,3,2,1,0:T(8,128)(2,1)S(1)}, bf16[1,2,1,144,1536]{4,3,2,1,0:T(8,128)(2,1)S(1)}, u32[]{:S(2)}, u32[]{:S(2)}) collective-permute-start(bf16[1,2,1,144,1536]{4,3,2,1,0:T(8,128)(2,1)S(1)} %maximum_select_fusion.10), channel_id=1, source_target_pairs={{0,8},{2,10},{4,12},{6,14},{8,0},{10,2},{12,4},{14,6},{16,24},{18,... | collective-permute-start | bytes 2654216 | tf_op jit(solution)/shard_map/ppermute | solution.py:925
  762.4 39.1 %collective-permute-start.68 = (bf16[1,1,2,192,1152]{4,3,2,1,0:T(8,128)(2,1)}, bf16[1,1,2,192,1152]{4,3,2,1,0:T(8,128)(2,1)}, u32[]{:S(2)}, u32[]{:S(2)}) collective-permute-start(bf16[1,1,2,192,1152]{4,3,2,1,0:T(8,128)(2,1)} %maximum_select_fusion.11), channel_id=1, source_target_pairs={{0,4},{2,6},{4,0},{6,2},{8,12},{10,14},{12,8},{14,10},{16,20},{18,... | collective-permute-start | bytes 2654216 | tf_op jit(solution)/shard_map/ppermute | solution.py:925
  765.2 43.3 %collective-permute-start.42 = (bf16[1,1,2,2,72,1152]{5,4,3,2,1,0:T(8,128)(2,1)}, bf16[1,1,2,2,72,1152]{5,4,3,2,1,0:T(8,128)(2,1)}, u32[]{:S(2)}, u32[]{:S(2)}) collective-permute-start(bf16[1,1,2,2,72,1152]{5,4,3,2,1,0:T(8,128)(2,1)} %maximum_select_fusion.15), channel_id=1, source_target_pairs={{0,2},{2,0},{4,6},{6,4},{8,10},{10,8},{12,14},{14,12},{16,18},{18,... | collective-permute-start | bytes 1990664 | tf_op jit(solution)/shard_map/ppermute | solution.py:925
  781.8 36.0 %collective-permute-start.60 = (bf16[576,2,768]{2,1,0:T(2,128)(2,1)}, bf16[576,2,768]{2,1,0:T(2,128)(2,1)}, u32[]{:S(2)}, u32[]{:S(2)}) collective-permute-start(bf16[576,2,768]{2,1,0:T(2,128)(2,1)} %select_n.1262), channel_id=1, source_target_pairs={{0,2},{2,0},{4,6},{6,4},{8,10},{10,8},{12,14},{14,12},{16,18},{18,... | collective-permute-start | bytes 5308424 | tf_op jit(solution)/shard_map/ppermute | solution.py:925
  787.8 56.6 %collective-permute-start.51 = (bf16[576,2,768]{2,1,0:T(2,128)(2,1)}, bf16[576,2,768]{2,1,0:T(2,128)(2,1)}, u32[]{:S(2)}, u32[]{:S(2)}) collective-permute-start(bf16[576,2,768]{2,1,0:T(2,128)(2,1)} %select_n.1253), channel_id=1, source_target_pairs={{0,2},{2,0},{4,6},{6,4},{8,10},{10,8},{12,14},{14,12},{16,18},{18,... | collective-permute-start | bytes 5308424 | tf_op jit(solution)/shard_map/ppermute | solution.py:925
  805.1 65.6 %collective-permute-start.69 = (bf16[768,1152]{1,0:T(8,128)(2,1)}, bf16[768,1152]{1,0:T(8,128)(2,1)}, u32[]{:S(2)}, u32[]{:S(2)}) collective-permute-start(bf16[768,1152]{1,0:T(8,128)(2,1)} %bitcast.70), channel_id=1, source_target_pairs={{0,2},{2,0},{4,6},{6,4},{8,10},{10,8},{12,14},{14,12},{16,18},{18,... | collective-permute-start | bytes 5308424 | tf_op jit(solution)/shard_map/ppermute | solution.py:925
  (78 other events, 850.1 us)

commit v3 on v2

--- a/solution.py
+++ b/solution.py
@@ -259,6 +259,285 @@
         name="fetch",
     )(inputs, eight(query), eight(key), eight(value), gains)
     return tokens, weight.reshape(16 * rows, total), both_gains
+
+
+AXES = ("y", "x", "zlo", "zhi")
+
+
+class Fold:
+    def __init__(self, source, kept, received, order, sems, slot, near, near_slot):
+        self.source, self.kept, self.received = source, kept, received
+        self.order, self.sems, self.slot = order, sems, slot
+        self.near, self.near_slot = near, near_slot
+
+    def pick(self, stage, bit):
+        left = [name for name in AXES if name not in self.order[:stage]]
+        return (slice(None),) * left.index(self.order[stage]) + (bit,)
+
+    def held(self, stage):
+        return self.source if stage == 0 else self.received[stage - 1]
+
+    def copy(self, stage):
+        name = self.order[stage]
+        source = self.held(stage).at[self.pick(stage, 1 - bit_of(name))]
+        return across(source, self.received[stage], self.sems, self.slot + stage, name)
+
+    def load(self):
+        source = self.source.at[self.pick(0, bit_of(self.order[0]))]
+        return pltpu.make_async_copy(source, self.kept, self.near.at[self.near_slot])
+
+    def begin(self):
+        self.copy(0).start()
+        if self.kept is not None:
+            self.load().start()
+
+    def advance(self, stage):
+        self.copy(stage).wait_recv()
+        target = self.received[stage]
+        lead = target.ndim - 2
+        if stage == 0 and self.kept is not None:
+            self.load().wait()
+            mine, at, bit = self.kept, 0, None
+        else:
+            bit = bit_of(self.order[stage])
+            mine, at = self.held(stage), len(self.pick(stage, 0)) - 1
+
+        @pl.loop(0, 2**lead)
+        def _(n):
+            index = tuple(n // 2 ** (lead - 1 - k) % 2 for k in range(lead))
+            from_ = index if bit is None else index[:at] + (bit,) + index[at:]
+            total = target[index].astype(jnp.float32) + mine[from_].astype(jnp.float32)
+            target[index] = low(total)
+
+        if stage + 1 < len(self.order):
+            self.copy(stage + 1).start()
+
+    def finish(self):
+        for stage in range(len(self.order)):
+            self.copy(stage).wait_send()
+
+
+class Rise:
+    def __init__(self, whole, order, columns, sems, slot):
+        self.whole, self.order, self.columns, self.sems, self.slot = whole, order, columns, sems, slot
+
+    def block(self, stage):
+        index = tuple(
+            slice(None) if name in self.order[:stage] else bit_of(name) for name in AXES[1:]
+        )
+        if self.whole.ndim == 6:
+            return [self.whole.at[(bit_of("core"),) + index]]
+        return [self.whole.at[index + (slice(None), columns)] for columns in self.columns]
+
+    def copies(self, stage, first=None):
+        blocks = self.block(stage)
+        count = len(blocks)
+        return [
+            across(
+                block if first is None else first,
+                block,
+                self.sems,
+                self.slot + stage * count + at,
+                self.order[stage],
+            )
+            for at, block in enumerate(blocks)
+        ]
+
+    def begin(self, first=None):
+        for copy in self.copies(0, first):
+            copy.start()
+
+    def advance(self, stage):
+        for copy in self.copies(stage):
+            copy.wait_recv()
+        if stage + 1 < len(self.order):
+            for copy in self.copies(stage + 1):
+                copy.start()
+
+    def finish(self):
+        for stage in range(len(self.order)):
+            for copy in self.copies(stage):
+                copy.wait_send()
+
+
+ORDERS = (("y", "x", "zlo", "zhi"), ("x", "zlo", "y", "zhi"), ("zlo", "y", "x", "zhi"))
+BACKS = (
+    ("zhi", "zlo", "x", "core"),
+    ("zhi", "x", "zlo", "core"),
+    ("zhi", "zlo", "x", "core"),
+)
+
+
+def hidden_columns(wide):
+    core = bit_of("core")
+    return [
+        pl.ds(pl.multiple_of(core * wide, WIDE), wide),
+        pl.ds(pl.multiple_of((2 + core) * wide, WIDE), wide),
+    ]
+
+
+def finish_body(term, gains, result, token_grad, gate_in, up_in, down_in,
+                gate, up, down, sums, outputs, input_grads, gain_sums,
+                r0, r1, r2, r3, r4, k0, gain_held, gain_came, rows_held, sems, near):
+    core, y = bit_of("core"), lax.axis_index("fsdp")
+    third = term.shape[-1] // 3
+    wide = third // 2
+    hidden = gate.shape[-1] // 4
+    columns = [
+        [pl.ds(pl.multiple_of(t * third + side * wide, WIDE), wide) for side in (core, 1 - core)]
+        for t in range(3)
+    ]
+    everything = (slice(None),) * 5
+    span = outputs.shape[1]
+    rows = [pl.ds(pl.multiple_of(at * span, span), span) for at in (y, 1 - y)]
+    loads = [
+        pltpu.make_async_copy(term.at[everything + (columns[t][0],)], k0.at[t], near.at[t])
+        for t in range(3)
+    ] + [
+        pltpu.make_async_copy(result.at[rows[0]], rows_held.at[0], near.at[3]),
+        pltpu.make_async_copy(token_grad.at[rows[0]], rows_held.at[1], near.at[4]),
+    ]
+    for load in loads:
+        load.start()
+    greet(("core", "y", "x", "zlo", "zhi"))
+    cores = [
+        across(term.at[everything + (columns[t][1],)], r0.at[t], sems, t, "core") for t in range(3)
+    ]
+    for copy in cores:
+        copy.start()
+    rises = [
+        Rise(gate, BACKS[0], hidden_columns(hidden), sems, 3),
+        Rise(up, BACKS[1], hidden_columns(hidden), sems, 11),
+        Rise(down, BACKS[2], None, sems, 19),
+    ]
+    folds = [
+        Fold(
+            r0.at[t], None, [r1.at[t], r2.at[t], r3.at[t], r4.at[t]], ORDERS[t], sems, 23 + 4 * t,
+            None, None,
+        )
+        for t in range(3)
+    ]
+    tops = [Rise(sums, BACKS[t], [columns[t][0]], sems, 35 + 4 * t) for t in range(3)]
+    swaps = [
+        across(result.at[rows[1]], outputs.at[y], sems, 52, "y"),
+        across(token_grad.at[rows[1]], input_grads.at[y], sems, 53, "y"),
+    ]
+    names = ("core",) + AXES
+    gain_copies = [
+        across(gain_held.at[at], gain_came.at[at], sems, 47 + at, name)
+        for at, name in enumerate(names)
+    ]
+    gain_held[0] = gains[...]
+    for rise in rises:
+        rise.begin()
+
+    def gain_step(at):
+        gain_copies[at].wait_recv()
+        gain_held[at + 1] = gain_held[at] + gain_came[at]
+        if at + 1 < len(names):
+            gain_copies[at + 1].start()
+
+    gain_copies[0].start()
+    for t in range(3):
+        cores[t].wait_recv()
+        loads[t].wait()
+
+        @pl.loop(0, 16)
+        def _(n, t=t):
+            index = (t, n // 8, n // 4 % 2, n // 2 % 2, n % 2)
+            r0[index] = low(r0[index].astype(jnp.float32) + k0[index].astype(jnp.float32))
+
+        folds[t].begin()
+    stores = [
+        pltpu.make_async_copy(rows_held.at[0], outputs.at[y], near.at[5]),
+        pltpu.make_async_copy(rows_held.at[1], input_grads.at[y], near.at[6]),
+    ]
+    for at in range(2):
+        swaps[at].start()
+        loads[3 + at].wait()
+        stores[at].start()
+    gain_step(0)
+    for t in range(3):
+        folds[t].advance(0)
+    gain_step(1)
+    for rise in rises:
+        rise.advance(0)
+    for t in range(3):
+        folds[t].advance(1)
+    gain_step(2)
+    for t in range(3):
+        folds[t].advance(2)
+    gain_step(3)
+    tops_here = []
+    for t in range(3):
+        folds[t].advance(3)
+        tops[t].begin(r4.at[t])
+        store = pltpu.make_async_copy(r4.at[t], tops[t].block(0)[0], near.at[7 + t])
+        store.start()
+        tops_here.append(store)
+    for rise in rises:
+        rise.advance(1)
+    for t in range(3):
+        tops_here[t].wait()
+        tops[t].advance(0)
+    gain_step(4)
+    for t in range(3):
+        tops[t].advance(1)
+    for rise in rises:
+        rise.advance(2)
+    for t in range(3):
+        tops[t].advance(2)
+    for rise in rises + tops:
+        rise.advance(3)
+    for copy in cores + swaps + gain_copies:
+        copy.wait_send()
+    for part in rises + tops + folds:
+        part.finish()
+    for copy in swaps:
+        copy.wait_recv()
+    for store in stores:
+        store.wait()
+    gain_sums[...] = gain_held[len(names)]
+
+
+def finish(term, gains, result, token_grad, gate, up, down):
+    length, width = result.shape
+    term = term.reshape(2, 2, 2, 2, term.shape[0] // 16, term.shape[1])
+    rows, total = term.shape[4:]
+    wide = total // 6
+    anywhere = pl.BlockSpec(memory_space=pl.ANY)
+    vmem = pl.BlockSpec(memory_space=pltpu.VMEM)
+    halves = jax.ShapeDtypeStruct((2, length // 2, width), result.dtype)
+    return pl.pallas_call(
+        finish_body,
+        in_specs=[anywhere, vmem] + [anywhere] * 5,
+        out_specs=[anywhere] * 6 + [vmem],
+        out_shape=[
+            jax.ShapeDtypeStruct(gate.shape, gate.dtype),
+            jax.ShapeDtypeStruct(up.shape, up.dtype),
+            jax.ShapeDtypeStruct(down.shape, down.dtype),
+            jax.ShapeDtypeStruct((2, 2, 2, rows, total), term.dtype),
+            halves,
+            halves,
+            jax.ShapeDtypeStruct(gains.shape, gains.dtype),
+        ],
+        input_output_aliases={4: 0, 5: 1, 6: 2},
+        scratch_shapes=[
+            pltpu.VMEM((3,) + (2,) * left + (rows, wide), jnp.bfloat16) for left in (4, 3, 2, 1, 0)
+        ]
+        + [
+            pltpu.VMEM((3, 2, 2, 2, 2, rows, wide), jnp.bfloat16),
+            pltpu.VMEM((6,) + gains.shape, jnp.float32),
+            pltpu.VMEM((5,) + gains.shape, jnp.float32),
+            pltpu.VMEM((2, length // 2, width), result.dtype),
+            pltpu.SemaphoreType.DMA((2, 54)),
+            pltpu.SemaphoreType.DMA((10,)),
+        ],
+        compiler_params=pltpu.CompilerParams(
+            collective_id=4, has_side_effects=True, vmem_limit_bytes=VMEM_MOST
+        ),
+        name="finish",
+    )(term, gains, result, token_grad, gate, up, down)
 
 
 def place_heads(tile, variants_ref):
@@ -454,10 +733,41 @@
 
 def attend_back_body(
     q_ref, k_ref, v_ref, grad_ref, mixed_ref, lse_ref, seg_col_ref, seg_row_ref, cos_ref, sin_ref,
-    dq_ref, dk_ref, dv_ref, ks, vs, kt, k_acc, v_acc, q_acc, sides, delta
+    gate_term, up_term, down_term,
+    dq_ref, dk_ref, dv_ref, gate_sum, up_sum, down_sum,
+    ks, vs, kt, k_acc, v_acc, q_acc, sides, delta, sems, near, kept, *received
 ):
     block = pl.program_id(1)
     length = k_ref.shape[0]
+    now = pl.program_id(0) * pl.num_programs(1) + block
+    most = pl.num_programs(0) * pl.num_programs(1) - 1
+    down_kept, down_received = received[4], received[5:]
+    folds = [
+        Fold(
+            term,
+            kept.at[at] if at < 2 else down_kept,
+            [r.at[at] for r in received[:4]] if at < 2 else list(down_received),
+            ORDERS[at],
+            sems,
+            4 * at,
+            near,
+            at,
+        )
+        for at, term in enumerate((gate_term, up_term, down_term))
+    ]
+
+    @pl.when(now == 0)
+    def _():
+        greet(AXES)
+        for fold in folds:
+            fold.begin()
+
+    for stage, at in ((0, 7), (1, 11)):
+
+        @pl.when(now == at)
+        def _(stage=stage):
+            for fold in folds:
+                fold.advance(stage)
 
     @pl.when(block == 0)
     def _():
@@ -532,9 +842,41 @@
             dk_ref[rows, :] = low(tile)
             dv_ref[rows, :] = low(gather(v_acc))
 
-
-def attend_back(qkv, mixed_grad, mixed, lse, seg_col, seg_row, cosines, sines):
+    @pl.when(now == most)
+    def _():
+        for stage in (2, 3):
+            for fold in folds:
+                fold.advance(stage)
+        place = tuple(bit_of(name) for name in AXES[1:])
+        wide = gate_sum.shape[-1] // 4
+        stores = [
+            pltpu.make_async_copy(
+                folds[at].received[3].at[:, half * wide : (half + 1) * wide],
+                whole.at[place + (slice(None), columns)],
+                near.at[3 + 2 * at + half],
+            )
+            for at, whole in enumerate((gate_sum, up_sum))
+            for half, columns in enumerate(hidden_columns(wide))
+        ]
+        stores.append(
+            pltpu.make_async_copy(
+                folds[2].received[3], down_sum.at[(bit_of("core"),) + place], near.at[7]
+            )
+        )
+        for store in stores:
+            store.start()
+        for fold in folds:
+            fold.finish()
+        for store in stores:
+            store.wait()
+
+
+def attend_back(qkv, mixed_grad, mixed, lse, seg_col, seg_row, cosines, sines, gate_term, up_term, down_term):
     length = qkv.shape[0]
+    terms = [t.reshape(2, 2, 2, 2, t.shape[0] // 16, t.shape[1]) for t in (gate_term, up_term, down_term)]
+    rows, wide = terms[0].shape[4:]
+    down_rows, width = terms[2].shape[4:]
+    anywhere = pl.BlockSpec(memory_space=pl.ANY)
     pairs = KV_HEADS // 2
     q_tiles = HEADS * HEAD // WIDE
     q_block = pl.BlockSpec((BLOCK, 3 * WIDE), lambda b, i: (i, b))
@@ -554,12 +896,16 @@
             pl.BlockSpec((1, BLOCK), lambda b, i: (0, i)),
             table,
             table,
-        ],
-        out_specs=[q_block, kv_block, kv_block],
+        ]
+        + [anywhere] * 3,
+        out_specs=[q_block, kv_block, kv_block] + [anywhere] * 3,
         out_shape=[
             jax.ShapeDtypeStruct((length, HEADS * HEAD), jnp.bfloat16),
             jax.ShapeDtypeStruct((length, KV_HEADS * HEAD), jnp.bfloat16),
             jax.ShapeDtypeStruct((length, KV_HEADS * HEAD), jnp.bfloat16),
+            jax.ShapeDtypeStruct((2, 2, 2, rows, 2 * wide), jnp.bfloat16),
+            jax.ShapeDtypeStruct((2, 2, 2, rows, 2 * wide), jnp.bfloat16),
+            jax.ShapeDtypeStruct((2, 2, 2, 2, down_rows, width), jnp.bfloat16),
         ],
         scratch_shapes=[
             pltpu.VMEM((4, length, WIDE), jnp.bfloat16),
@@ -570,14 +916,202 @@
             pltpu.VMEM((6 * HEAD, BLOCK), jnp.float32),
             pltpu.VMEM((2, 3, 2 * BLOCK, WIDE), jnp.bfloat16),
             pltpu.VMEM((8, BLOCK), jnp.float32),
-        ],
+            pltpu.SemaphoreType.DMA((2, 12)),
+            pltpu.SemaphoreType.DMA((8,)),
+        ]
+        + [pltpu.VMEM((2,) + (2,) * left + (rows, wide), jnp.bfloat16) for left in (3, 3, 2, 1, 0)]
+        + [pltpu.VMEM((2,) * left + (down_rows, width), jnp.bfloat16) for left in (3, 3, 2, 1, 0)],
+        compiler_params=pltpu.CompilerParams(
+            collective_id=3, has_side_effects=True, vmem_limit_bytes=VMEM_MOST
+        ),
         cost_estimate=pl.CostEstimate(
             flops=40 * length * length * HEADS * HEAD // 2,
             bytes_accessed=12 * length * HEADS * HEAD,
             transcendentals=HEADS * length * length // 2,
         ),
         name="attend_back",
-    )(qkv, qkv, qkv, mixed_grad, mixed, lse, seg_col, seg_row, cosines, sines)
+    )(qkv, qkv, qkv, mixed_grad, mixed, lse, seg_col, seg_row, cosines, sines, *terms)
+
+
+def mix_body(x_ref, mixed_ref, w_ref, gain_ref, residual_ref, normed_ref, turned_ref):
+    residual = x_ref[...].astype(jnp.float32) + mm(mixed_ref[...], w_ref[...])
+    residual_ref[...] = residual
+    inverse = lax.rsqrt(jnp.mean(residual * residual, axis=-1, keepdims=True) + epsilon)
+    normed = residual * inverse * gain_ref[...]
+    normed_ref[...] = low(normed)
+    turned_ref[...] = low(normed.T)
+
+
+def mix(x, mixed, w, gain):
+    length, width = x.shape
+    rows = pl.BlockSpec((BLOCK, width), lambda i: (i, 0))
+    return pl.pallas_call(
+        mix_body,
+        grid=(length // BLOCK,),
+        in_specs=[
+            rows,
+            rows,
+            pl.BlockSpec(w.shape, lambda i: (0, 0), pipeline_mode=pl.Buffered(1)),
+            pl.BlockSpec((1, width), lambda i: (0, 0)),
+        ],
+        out_specs=[rows, rows, pl.BlockSpec((width, BLOCK), lambda i: (0, i))],
+        out_shape=[
+            jax.ShapeDtypeStruct((length, width), jnp.float32),
+            jax.ShapeDtypeStruct((length, width), jnp.bfloat16),
+            jax.ShapeDtypeStruct((width, length), jnp.bfloat16),
+        ],
+        cost_estimate=pl.CostEstimate(
+            flops=2 * length * width * width, bytes_accessed=12 * length * width, transcendentals=0
+        ),
+        name="mix",
+    )(x, mixed, w, gain)
+
+
+def norm_grad(grad, gain, scaled, inverse):
+    weighted = grad * gain
+    return inverse * (weighted - scaled * jnp.mean(weighted * scaled, axis=-1, keepdims=True))
+
+
+def turn_body(residual_ref, out_a, out_b, back_a, back_b, c_ref, mixed_ref, w_ref, gain_ref,
+              result_ref, grad_ref, mixed_grad_ref, term_ref, gain_term_ref, total):
+    step = pl.program_id(0)
+    residual = residual_ref[...]
+    result_ref[...] = low(residual + out_a[...] + out_b[...])
+    inverse = lax.rsqrt(jnp.mean(residual * residual, axis=-1, keepdims=True) + epsilon)
+    scaled = residual * inverse
+    normed_grad = back_a[...] + back_b[...]
+    gain_term = jnp.sum(normed_grad * scaled, axis=0, keepdims=True)
+    grad = c_ref[...].astype(jnp.float32) + norm_grad(normed_grad, gain_ref[...], scaled, inverse)
+    grad_ref[...] = grad
+    grad_low = low(grad)
+    mixed_grad_ref[...] = low(mm_nt(grad_low, w_ref[...]))
+    term = mm_tn(mixed_ref[...], grad_low)
+
+    @pl.when(step == 0)
+    def _():
+        total[...] = term
+        gain_term_ref[...] = jnp.broadcast_to(gain_term, gain_term_ref.shape)
+
+    @pl.when(step > 0)
+    def _():
+        total[...] += term
+        gain_term_ref[...] += jnp.broadcast_to(gain_term, gain_term_ref.shape)
+
+    @pl.when(step == pl.num_programs(0) - 1)
+    def _():
+        term_ref[...] = low(total[...])
+
+
+def turn(residual, out_a, out_b, back_a, back_b, c, mixed, w, gain):
+    length, width = residual.shape
+    rows = pl.BlockSpec((BLOCK, width), lambda i: (i, 0))
+    whole = lambda shape: pl.BlockSpec(shape, lambda i: (0, 0), pipeline_mode=pl.Buffered(1))
+    return pl.pallas_call(
+        turn_body,
+        grid=(length // BLOCK,),
+        in_specs=[rows] * 7 + [whole(w.shape), pl.BlockSpec((1, width), lambda i: (0, 0))],
+        out_specs=[
+            rows, rows, rows, whole((width, width)), pl.BlockSpec((8, width), lambda i: (0, 0)),
+        ],
+        out_shape=[
+            jax.ShapeDtypeStruct((length, width), jnp.bfloat16),
+            jax.ShapeDtypeStruct((length, width), jnp.float32),
+            jax.ShapeDtypeStruct((length, width), jnp.bfloat16),
+            jax.ShapeDtypeStruct((width, width), jnp.bfloat16),
+            jax.ShapeDtypeStruct((8, width), jnp.float32),
+        ],
+        scratch_shapes=[pltpu.VMEM((width, width), jnp.float32)],
+        compiler_params=pltpu.CompilerParams(vmem_limit_bytes=VMEM_MOST),
+        cost_estimate=pl.CostEstimate(
+            flops=4 * length * width * width, bytes_accessed=32 * length * width, transcendentals=0
+        ),
+        name="turn",
+    )(residual, out_a, out_b, back_a, back_b, c, mixed, w, gain)
+
+
+def close_body(dq_ref, dk_ref, dv_ref, normed_ref, x_ref, grad_ref, w_ref, gain_ref, mix_term_ref,
+               term_ref, token_grad_ref, gain_term_ref, turned):
+    step = pl.program_id(0)
+    rows_each = x_ref.shape[0]
+    length = normed_ref.shape[0]
+    q_width, k_width = dq_ref.shape[1], dk_ref.shape[1]
+
+    @pl.when(step == 0)
+    def _():
+        for at in range(0, length, BLOCK):
+            turned[:, at : at + BLOCK] = normed_ref[at : at + BLOCK, :].T
+
+    for chunk in range(3):
+
+        @pl.when(step == chunk)
+        def _(chunk=chunk):
+            at = chunk * k_width
+            term_ref[...] = low(mm(turned[...], dq_ref[:, at : at + k_width]))
+
+    @pl.when(step == 3)
+    def _():
+        term_ref[...] = low(mm(turned[...], dk_ref[...]))
+
+    @pl.when(step == 4)
+    def _():
+        term_ref[...] = low(mm(turned[...], dv_ref[...]))
+
+    @pl.when(step > 4)
+    def _():
+        term_ref[...] = mix_term_ref[...]
+
+    rows = pl.ds(pl.multiple_of(step * rows_each, rows_each), rows_each)
+    normed_grad = (
+        mm_nt(dq_ref[rows, :], w_ref[:, :q_width])
+        + mm_nt(dk_ref[rows, :], w_ref[:, q_width : q_width + k_width])
+        + mm_nt(dv_ref[rows, :], w_ref[:, q_width + k_width :])
+    )
+    values = x_ref[...].astype(jnp.float32)
+    inverse = lax.rsqrt(jnp.mean(values * values, axis=-1, keepdims=True) + epsilon)
+    scaled = values * inverse
+    gain_term = jnp.sum(normed_grad * scaled, axis=0, keepdims=True)
+    token_grad_ref[...] = low(
+        grad_ref[...] + norm_grad(normed_grad, gain_ref[...], scaled, inverse)
+    )
+
+    @pl.when(step == 0)
+    def _():
+        gain_term_ref[...] = jnp.broadcast_to(gain_term, gain_term_ref.shape)
+
+    @pl.when(step > 0)
+    def _():
+        gain_term_ref[...] += jnp.broadcast_to(gain_term, gain_term_ref.shape)
+
+
+def close(dq, dk, dv, normed, x, grad, w, gain, mix_term):
+    length, width = x.shape
+    k_width = dk.shape[1]
+    steps = (w.shape[1] + mix_term.shape[1]) // k_width
+    rows = pl.BlockSpec((length // steps, width), lambda i: (i, 0))
+    whole = lambda a: pl.BlockSpec(a.shape, lambda i: (0, 0), pipeline_mode=pl.Buffered(1))
+    return pl.pallas_call(
+        close_body,
+        grid=(steps,),
+        in_specs=[whole(dq), whole(dk), whole(dv), whole(normed), rows, rows, whole(w),
+                  pl.BlockSpec((1, width), lambda i: (0, 0)),
+                  pl.BlockSpec((width, k_width), lambda i: (0, jnp.maximum(i - 5, 0)))],
+        out_specs=[
+            pl.BlockSpec((width, k_width), lambda i: (0, i)),
+            rows,
+            pl.BlockSpec((8, width), lambda i: (0, 0)),
+        ],
+        out_shape=[
+            jax.ShapeDtypeStruct((width, steps * k_width), jnp.bfloat16),
+            jax.ShapeDtypeStruct((length, width), jnp.bfloat16),
+            jax.ShapeDtypeStruct((8, width), jnp.float32),
+        ],
+        scratch_shapes=[pltpu.VMEM((width, length), jnp.bfloat16)],
+        compiler_params=pltpu.CompilerParams(vmem_limit_bytes=VMEM_MOST),
+        cost_estimate=pl.CostEstimate(
+            flops=4 * length * width * w.shape[1], bytes_accessed=24 * length * width, transcendentals=0
+        ),
+        name="close",
+    )(dq, dk, dv, normed, x, grad, w, gain, mix_term)
 
 
 def feed_body(which_ref, normed_ref, turned_ref, c_ref, gate_ref, up_ref, down_ref,
@@ -945,25 +1479,6 @@
     )
 
 
-def reduce_down(places, terms, stages):
-    for name, axis in stages:
-        bit = places.bit(name)
-        sent = add_up([part_of(term, axis, 1 - bit) for term in terms])
-        terms = [part_of(term, axis, bit) for term in terms] + [places.swap(sent, name)]
-    return add_up(terms)
-
-
-def gather_up(places, piece, stages):
-    for name, axis in stages:
-        piece = in_order(places.bit(name), piece, places.swap(piece, name), axis)
-    return piece
-
-
-def norm_grad(grad, gain, scaled, inverse):
-    weighted = grad * gain
-    return inverse * (weighted - scaled * jnp.mean(weighted * scaled, axis=-1, keepdims=True))
-
-
 def paired_local(
     group_size,
     inputs,
@@ -984,11 +1499,6 @@
     span, length, width = inputs.shape[1], segments.shape[1], inputs.shape[2]
     q_width = query_weight.shape[1]
 
-    def own_blocks(rows):
-        own = part_of(rows, 0, y)
-        other = places.swap(part_of(rows, 0, 1 - y), "y")
-        return in_order(y, own[None], other[None], 0)
-
     gains = jnp.pad(
         jnp.stack([attention_gain, feedforward_gain]).astype(jnp.float32), ((0, 6), (0, 0))
     )
@@ -1004,99 +1514,42 @@
         qkv, seg_col, seg_row, out_grad, output_weight, gate_weight, up_weight, down_weight
     )
 
-    values = tokens.astype(jnp.float32)
-    residual = values + mm(mixed, mix_weight)
-    inverse_f = lax.rsqrt(jnp.mean(residual * residual, axis=-1, keepdims=True) + epsilon)
-    normed_f = low(residual * inverse_f * gain_f)
-    turned_f = normed_f.T
+    residual, normed_f, turned_f = mix(tokens, mixed, mix_weight, gain_f)
 
     core = places.bit("core")
     theirs = feed((1 - core).reshape(1), normed_f, turned_f, c, full_gate, full_up, full_down)
+    came = [places.swap(term, "core") for term in theirs[2:]]
     mine = feed(core.reshape(1), normed_f, turned_f, c, full_gate, full_up, full_down)
-    result = low(residual + theirs[0] + mine[0])
-    outputs = own_blocks(result)
-
-    normed_f_grad = theirs[1] + mine[1]
-    scaled_f = residual * inverse_f
-    feed_gain_term = jnp.sum(normed_f_grad * scaled_f, axis=0)
-    residual_grad = c.astype(jnp.float32) + norm_grad(normed_f_grad, gain_f, scaled_f, inverse_f)
-    residual_low = low(residual_grad)
-    mix_term = low(mm_tn(mixed, residual_low))
-    mixed_grad = low(mm_nt(residual_low, mix_weight))
-
-    orders = (("y", "x", "zlo", "zhi"), ("x", "zlo", "y", "zhi"), ("zlo", "y", "x", "zhi"))
-    backs = (("zhi", "zlo", "x"), ("zhi", "x", "zlo"), ("zhi", "zlo", "x"))
-    dims = {"y": 0, "x": 1, "zlo": 2, "zhi": 3}
-    pieces = []
-    for index in range(3):
-        shape = mine[2 + index].shape
-        split = (2, 2, 2, shape[0] // 8, shape[1])
-        terms = [mine[2 + index].reshape(split), places.swap(theirs[2 + index], "core").reshape(split)]
-        piece = reduce_down(places, terms, [(name, dims[name]) for name in orders[index]])
-        pieces.append(gather_up(places, piece, [(name, dims[name]) for name in backs[index]]))
-
-    def hidden_columns(piece):
-        wide = piece.shape[-1] // 2
-        piece = piece.reshape(width // 2, 2, wide)
-        other = places.swap(piece, "core")
-        return in_order(core, piece[:, :, None], other[:, :, None], 2).reshape(width // 2, 4 * wide)
-
-    gate_sum_grad = hidden_columns(pieces[0]).astype(jnp.float32)
-    up_sum_grad = hidden_columns(pieces[1]).astype(jnp.float32)
-    down_piece = pieces[2].reshape(-1, width)
-    down_sum_grad = in_order(core, down_piece, places.swap(down_piece, "core"), 0).astype(jnp.float32)
-
-    dq, dk, dv = attend_back(qkv, mixed_grad, mixed, lse, seg_col, seg_row, cosines, sines)
-    lows = jnp.concatenate([dq, dk, dv], axis=1)
-    qkv_term = low(mm_tn(normed_a, lows))
-    normed_a_grad = mm_nt(lows, qkv_weight)
-    inverse_a = lax.rsqrt(jnp.mean(values * values, axis=-1, keepdims=True) + epsilon)
-    scaled_a = values * inverse_a
-    attention_gain_term = jnp.sum(normed_a_grad * scaled_a, axis=0)
-    token_grad = low(residual_grad + norm_grad(normed_a_grad, gain_a, scaled_a, inverse_a))
-    input_grads = own_blocks(token_grad)
-
-    dims = {"y": 0, "core": 1, "x": 2, "zlo": 3, "zhi": 4}
-
-    def whole_sum(term, order, back):
-        term = term.reshape(2, 2, 2, 2, term.shape[0] // 16, term.shape[1])
-        piece = reduce_down(places, [term], [(name, dims[name]) for name in order])
-        piece = gather_up(places, piece, [(name, dims[name]) for name in back])
-        return piece.reshape(-1, piece.shape[-1])
-
-    mix_sum_grad = whole_sum(
-        mix_term, ("core", "x", "y", "zlo", "zhi"), ("zhi", "zlo", "x", "core")
-    ).astype(jnp.float32)
-    third = qkv_term.shape[1] // 3
-    qkv_sum = jnp.concatenate(
-        [
-            whole_sum(
-                qkv_term[:, i * third : (i + 1) * third],
-                ("core",) + orders[i],
-                backs[i] + ("core",),
-            )
-            for i in range(3)
-        ],
-        axis=1,
-    ).astype(jnp.float32)
-
-    gain_terms = jnp.stack([attention_gain_term, feed_gain_term])
-    for name in ("core", "y", "x", "zlo", "zhi"):
-        gain_terms = gain_terms + places.swap(gain_terms, name)
-    gain_grads = part_of(gain_terms, 1, y)
+    hidden_terms = [add_up([own, other]) for own, other in zip(mine[2:], came)]
+    result, residual_grad, mixed_grad, mix_term, feed_gain_term = turn(
+        residual, theirs[0], mine[0], theirs[1], mine[1], c, mixed, mix_weight, gain_f
+    )
+    dq, dk, dv, gate_sum, up_sum, down_sum = attend_back(
+        qkv, mixed_grad, mixed, lse, seg_col, seg_row, cosines, sines, *hidden_terms
+    )
+    term, token_grad, attention_gain_term = close(
+        dq, dk, dv, normed_a, tokens, residual_grad, qkv_weight, gain_a, mix_term
+    )
+    gain_terms = jnp.concatenate(
+        [attention_gain_term[0:1], feed_gain_term[0:1], jnp.zeros_like(gains[2:])], axis=0
+    )
+    gate_sum, up_sum, down_sum, sums, outputs, input_grads, gain_sums = finish(
+        term, gain_terms, result, token_grad, gate_sum, up_sum, down_sum
+    )
+    gain_grads = lax.dynamic_slice_in_dim(gain_sums, y * (width // 2), width // 2, 1)
     k_width = key_weight.shape[1]
+    sums = sums.reshape(width // 2, -1).astype(jnp.float32)
+    ends = (0, q_width, q_width + k_width, q_width + 2 * k_width, sums.shape[1])
+    parts = [sums[:, a:b] for a, b in zip(ends[:-1], ends[1:])]
     return (
         outputs,
         input_grads,
         gain_grads[0],
-        qkv_sum[:, :q_width],
-        qkv_sum[:, q_width : q_width + k_width],
-        qkv_sum[:, q_width + k_width :],
-        mix_sum_grad,
+        *parts,
         gain_grads[1],
-        gate_sum_grad,
-        up_sum_grad,
-        down_sum_grad,
+        gate_sum.reshape(width // 2, -1).astype(jnp.float32),
+        up_sum.reshape(width // 2, -1).astype(jnp.float32),
+        down_sum.reshape(-1, width).astype(jnp.float32),
     )
 
 

time: 889 us -> 638 us (0.72)
  Pallas kernels: 296 us -> 574 us
  waiting for transfers between devices: 251 us -> 0.01 us
  local copies, waits for them, and re-layouts: 124 us -> 17.4 us
  other arithmetic: 114 us -> 35.7 us
  starting transfers between devices: 55.5 us -> 0.89 us
  matrix products: 35.8 us -> 0 us
    pallas_call x0 -> x4, Pallas kernels: none -> 224 us  [the longest x1 168 us: finish(): pl.pallas_call(finish_body, in_specs=[anywhere, vmem] + [anywhere] * 5, o...]
    ppermute x60 -> x3, waiting for transfers between devices: 192 us -> 0.01 us  [swap(): lax.ppermute(array, 'group', [(i, i ^ mask) for i in range(self.size)])]
    ppermute x10 -> x0, waiting for transfers between devices: 59.3 us -> none  [swap(): return lax.ppermute(array, 'fsdp', [(0, 1), (1, 0)])]
    convert_element_type x5 -> x0, local copies, waits for them, and re-layouts: 45.2 us -> none  [the longest x2 21.6 us: paired_local(): up_sum_grad = hidden_columns(pieces[1]).astype(jnp.float32)]
    pallas_call x1, Pallas kernels: 69.4 us -> 111 us  [attend_back(): pl.pallas_call(attend_back_body, grid=(pairs, length // BLOCK), in_specs=...]
    ppermute x60 -> x3, starting transfers between devices: 42 us -> 0.89 us  [swap(): lax.ppermute(array, 'group', [(i, i ^ mask) for i in range(self.size)])]
    dot_general x5 -> x0, matrix products: 35.8 us -> none  [the longest x2 15.3 us: mm_nt(): lax.dot_general(left, right, (((1,), (1,)), ((), ())), preferred_element_...]
    pallas_call x6 -> x0, local copies, waits for them, and re-layouts: 33.1 us -> none  [the longest x4 24.4 us: feed(): pl.pallas_call(feed_body, grid_spec=pltpu.PrefetchScalarGridSpec(num_scal...]
  transfers between devices with their start and end apart: 70 -> 3, of which waited for: 37 -> 0; matrix products, arithmetic and copies ran while one was open for 19% -> 2% of each run, Pallas kernels for 0% -> 12%
where the time goes in v3:
time: 638 us; the launch traced here: 628 us
  Pallas kernels  574 us (90%)
  other arithmetic  35.7 us (6%)
  local copies, waits for them, and re-layouts  17.4 us (3%)
    pallas_call x1, Pallas kernels, finish(): pl.pallas_call(finish_body, in_specs=[anywhere, vmem] + [anywhere] * 5, o...  168 us
    pallas_call x1, Pallas kernels, attend_back(): pl.pallas_call(attend_back_body, grid=(pairs, length // BLOCK), in_specs=...  111 us
    pallas_call x2, Pallas kernels, feed(): pl.pallas_call(feed_body, grid_spec=pltpu.PrefetchScalarGridSpec(num_scal...  103 us
    pallas_call x1, Pallas kernels, attend(): pl.pallas_call(attend_body, grid=(pairs, length // BLOCK), in_specs=[pl.B...  86.3 us
    pallas_call x1, Pallas kernels, fetch(): pl.pallas_call(fetch_body, in_specs=[anywhere] * 5, out_specs=[anywhere]...  37.2 us
    pallas_call x1, Pallas kernels, close(): pl.pallas_call(close_body, grid=(steps,), in_specs=[whole(dq), whole(dk),...  26.9 us
    pallas_call x1, Pallas kernels, turn(): pl.pallas_call(turn_body, grid=(length // BLOCK,), in_specs=[rows] * 7 +...  20.2 us
    convert_element_type x3, other arithmetic, low(): return values.astype(jnp.bfloat16)  15.7 us
  transfers between devices with their start and end apart: 3, of which 0 were waited for; matrix products, arithmetic and copies ran while one was open for 2% of the time, Pallas kernels for 12%

profile of v3, /device:TPU:0, one launch (start us, length us, event | category | flops | bytes accessed | tf_op | source)
XLA Modules:
  0.0 628.5 jit_solution(14590545093132407860)
XLA Ops:
  4.0 37.2 %fetch.1 = (bf16[1024,1152]{1,0:T(8,128)(2,1)}, bf16[16,72,1920]{2,1,0:T(8,128)(2,1)}, f32[2,8,576]{2,1,0:T(8,128)}) custom-call(bf16[2,512,1152]{2,1,0:T(8,128)(2,1)} %inputs.1, bf16[8,72,1152]{2,1,0:T(8,128)(2,1)} %bitcast.39, bf16[8,72,384]{2,1,0:T(8,128)(2,1)} %bitcast.40, bf16[8,72,384]{2,1,0:T(8,128)(2,1)} %bitcast.41, f32[8,576]{1,0:T(8,128)} %fusion.6.gains), custom_call_target="tpu_custom_call" | custom-call | tf_op jit(solution)/shard_map/fetch/pallas_call | solution.py:243
  42.7 2.0 fusion.2
  46.4 1.8 pad_maximum_fusion
  48.2 11.4 %project.1 = (bf16[1024,1152]{1,0:T(8,128)(2,1)}, bf16[1024,1920]{1,0:T(8,128)(2,1)}) custom-call(bf16[1024,1152]{1,0:T(8,128)(2,1)} %get-tuple-element.57.x_ref, f32[1,1152]{1,0:T(1,128)} %slice.37.gain_ref, bf16[1152,1920]{1,0:T(8,128)(2,1)} %bitcast.43, f32[1024,128]{1,0:T(8,128)} %get-tuple-element.114.cos_ref, f32[1024,128]{1,0:T(8,128)} %get-tuple-element.115.sin_ref), custom_call_target="tpu_custom_call" | custom-call | flops 4529848320 | bytes 13074432 | tf_op jit(solution)/shard_map/project/pallas_call | solution.py:90
  59.6 86.3 %attend.1 = (bf16[1024,1152]{1,0:T(8,128)(2,1)}, f32[3,8,1024]{2,1,0:T(8,128)}, bf16[1024,1152]{1,0:T(8,128)(2,1)}, bf16[16,72,1152]{2,1,0:T(8,128)(2,1)}, bf16[...) custom-call(bf16[1024,1920]{1,0:T(8,128)(2,1)} %get-tuple-element.60.q_ref.k_ref.v_ref, ...), custom_call_target="tpu_custom_call" | custom-call | flops 9663676416 | bytes 7077888 | tf_op jit(solution)/shard_map/attend/pallas_call | solution.py:689
  146.0 9.5 %mix.1 = (f32[1024,1152]{1,0:T(8,128)}, bf16[1024,1152]{1,0:T(8,128)(2,1)}, bf16[1152,1024]{1,0:T(8,128)(2,1)}) custom-call(bf16[1024,1152]{1,0:T(8,128)(2,1)} %get-tuple-element.57.x_ref, bf16[1024,1152]{1,0:T(8,128)(2,1)} %get-tuple-element.61.mixed_ref, bf16[1152,1152]{1,0:T(8,128)(2,1)} %bitcast.37, f32[1,1152]{1,0:T(1,128)} %slice.39.gain_ref), custom_call_target="tpu_custom_call" | custom-call | flops 2717908992 | bytes 14155776 | tf_op jit(solution)/shard_map/mix/pallas_call | solution.py:948
  155.5 45.7 %feed.2 = (f32[1024,1152]{1,0:T(8,128)}, f32[1024,1152]{1,0:T(8,128)}, bf16[1152,1536]{1,0:T(8,128)(2,1)}, bf16[1152,1536]{1,0:T(8,128)(2,1)}, bf16[1536,1152]{1,0:T(8,128)(2,1)}) custom-call(s32[1]{0:T(128)} %bitcast.11.which_ref, bf16[1024,1152]{1,0:T(8,128)(2,1)} %get-tuple-element.64.normed_ref, bf16[1152,1024]{1,0:T(8,128)(2,1)} %get-tuple-element.65.turned_ref, ...), custom_call_target="tpu_custom_call" | custom-call | flops 32614907904 | bytes 40108032 | tf_op jit(solution)/shard_map/feed/pallas_call | solution.py:1160
  202.1 57.2 %feed.3 = (f32[1024,1152]{1,0:T(8,128)}, f32[1024,1152]{1,0:T(8,128)}, bf16[1152,1536]{1,0:T(8,128)(2,1)}, bf16[1152,1536]{1,0:T(8,128)(2,1)}, bf16[1536,1152]{1,0:T(8,128)(2,1)}) custom-call(s32[1]{0:T(128)} %bitcast.15.which_ref, bf16[1024,1152]{1,0:T(8,128)(2,1)} %get-tuple-element.64.normed_ref, bf16[1152,1024]{1,0:T(8,128)(2,1)} %get-tuple-element.65.turned_ref, ...), custom_call_target="tpu_custom_call" | custom-call | flops 32614907904 | bytes 40108032 | tf_op jit(solution)/shard_map/feed/pallas_call | solution.py:1160
  259.3 20.2 %turn.1 = (bf16[1024,1152]{1,0:T(8,128)(2,1)}, f32[1024,1152]{1,0:T(8,128)}, bf16[1024,1152]{1,0:T(8,128)(2,1)}, bf16[1152,1152]{1,0:T(8,128)(2,1)}, f32[8,1152]{1,0:T(8,128)}) custom-call(f32[1024,1152]{1,0:T(8,128)} %get-tuple-element.63.residual_ref, f32[1024,1152]{1,0:T(8,128)} %get-tuple-element.70.out_a, f32[1024,1152]{1,0:T(8,128)} %get-tuple-element.71.out_b, ...), custom_call_target="tpu_custom_call" | custom-call | flops 5435817984 | bytes 37748736 | tf_op jit(solution)/shard_map/turn/pallas_call | solution.py:1009
  280.4 6.0 add_convert_fusion.2
  286.4 5.0 add_convert_fusion.1
  291.4 4.8 add_convert_fusion
  296.2 111.4 %attend_back.1 = (bf16[1024,1152]{1,0:T(8,128)(2,1)}, bf16[1024,384]{1,0:T(8,128)(2,1)}, bf16[1024,384]{1,0:T(8,128)(2,1)}, bf16[2,2,2,72,3072]{4,3,2,1,0:T(8,12...) custom-call(bf16[1024,1920]{1,0:T(8,128)(2,1)} %get-tuple-element.60.q_ref.k_ref.v_ref, ...), custom_call_target="tpu_custom_call" | custom-call | flops 24159191040 | bytes 14155776 | tf_op jit(solution)/shard_map/attend_back/pallas_call | solution.py:885
  407.6 26.9 %close.1 = (bf16[1152,3072]{1,0:T(8,128)(2,1)}, bf16[1024,1152]{1,0:T(8,128)(2,1)}, f32[8,1152]{1,0:T(8,128)}) custom-call(bf16[1024,1152]{1,0:T(8,128)(2,1)} %get-tuple-element.82.dq_ref, bf16[1024,384]{1,0:T(8,128)(2,1)} %get-tuple-element.83.dk_ref, bf16[1024,384]{1,0:T(8,128)(2,1)} %get-tuple-element.84.dv_ref, ...), custom_call_target="tpu_custom_call" | custom-call | flops 9059696640 | bytes 28311552 | tf_op jit(solution)/shard_map/close/pallas_call | solution.py:1092
  436.0 167.6 %finish.1 = (bf16[2,2,2,72,3072]{4,3,2,1,0:T(8,128)(2,1)}, bf16[2,2,2,72,3072]{4,3,2,1,0:T(8,128)(2,1)}, bf16[2,2,2,2,96,1152]{5,4,3,2,1,0:T(8,128)(2,1)}, bf16[...) custom-call(bf16[2,2,2,2,72,3072]{5,4,3,2,1,0:T(8,128)(2,1)} %bitcas, ...), custom_call_target="tpu_custom_call", output_to_operand_aliasing={{0}: (4, {}), {1}: (5, {}), {2}: (6, {})} | custom-call | tf_op jit(solution)/shard_map/finish/pallas_call | solution.py:511
  603.6 2.9 bitcast_convert_fusion.3
  606.5 2.8 fusion.7
  609.3 1.3 fusion.8
  611.9 4.1 bitcast_convert_fusion.2
  616.1 4.1 bitcast_convert_fusion.1
  620.2 3.7 bitcast_convert_fusion
  623.9 1.6 dynamic-slice_reduce_fusion
  625.5 1.4 copy.33
  626.9 1.4 copy.34
  (39 shorter events, 11.1 us)
Async XLA Ops:
  0.6 0.7 copy-start
  201.2 79.2 %collective-permute-start = (bf16[1152,1536]{1,0:T(8,128)(2,1)}, bf16[1152,1536]{1,0:T(8,128)(2,1)}, u32[]{:S(2)}, u32[]{:S(2)}) collective-permute-start(bf16[1152,1536]{1,0:T(8,128)(2,1)} %get-tuple-element.77), channel_id=1, source_target_pairs={{0,2},{2,0},{4,6},{6,4},{8,10},{10,8},{12,14},{14,12},{16,18},{18,... | collective-permute-start | bytes 10616840 | tf_op jit(solution)/shard_map/ppermute | solution.py:1459
  201.6 84.8 %collective-permute-start.1 = (bf16[1152,1536]{1,0:T(8,128)(2,1)}, bf16[1152,1536]{1,0:T(8,128)(2,1)}, u32[]{:S(2)}, u32[]{:S(2)}) collective-permute-start(bf16[1152,1536]{1,0:T(8,128)(2,1)} %get-tuple-element.79), channel_id=1, source_target_pairs={{0,2},{2,0},{4,6},{6,4},{8,10},{10,8},{12,14},{14,12},{16,18},{18,... | collective-permute-start | bytes 10616840 | tf_op jit(solution)/shard_map/ppermute | solution.py:1459
  201.7 89.7 %collective-permute-start.2 = (bf16[1536,1152]{1,0:T(8,128)(2,1)}, bf16[1536,1152]{1,0:T(8,128)(2,1)}, u32[]{:S(2)}, u32[]{:S(2)}) collective-permute-start(bf16[1536,1152]{1,0:T(8,128)(2,1)} %get-tuple-element.81), channel_id=1, source_target_pairs={{0,2},{2,0},{4,6},{6,4},{8,10},{10,8},{12,14},{14,12},{16,18},{18,... | collective-permute-start | bytes 10616840 | tf_op jit(solution)/shard_map/ppermute | solution.py:1459
  280.4 6.0 copy-start.6
  286.4 5.0 copy-start.5
  609.3 2.6 copy-start.2
  611.9 4.1 copy-start.3
  616.1 4.1 copy-start.4
  620.2 5.3 copy-start.8
  623.9 3.0 copy-start.7
  625.5 2.8 copy-start.1
